TPU v7x, 32 devices: a whole 2x2x4 slice. The times are simulated.
32 devices in a mesh: row: 8 (over y, x, core), col: 4 (over z).
Axes of the slice: x: 2, y: 2, z: 4, core: 2. Of those that a mesh axis runs over, the one named last changes fastest.
Arguments:
- start_vectors: bfloat16 [16384, 128], P(('row', 'col')), may hold values from -6 to 6
- tiles: bfloat16 [8, 128, 128, 128], P('row', 'col'), may hold values from -0.09375 to 0.09375
- tile_rows: int32 [8, 128], P('row', 'col'), may hold values from 0 to 15, as said below
- tile_cols: int32 [8, 128], P('row', 'col'), may hold values from 0 to 19
- tile_counts: int32 [8, 4], P('row', 'col'), may hold values from 4 to 32, as said below
- center: float32 [1], replicated, may hold values from -1 to 1
- half_width: float32 [1], replicated, may hold values from 2 to 3
Outputs:
- filtered: bfloat16 [16384, 128], P(('row', 'col'))
Inputs may be any that keep to these rules, and one draw needn't show every extreme that they name: On each device the 32 slots name different places (tile_rows, tile_cols); only the first tile_counts slots are in use. `tile_counts`: some device uses exactly 32 slots.
All inputs are finite; a program needn't handle non-finite values.
Results may differ from a plain program's by a relative error of at most 0.009.
Values may be sent and summed in bfloat16 or wider, within the bound.
A program may use at most 64 MiB of HBM per device.

v0:
```python
import functools

import jax
import jax.numpy as jnp
from jax import lax
from jax.experimental import pallas as pl
from jax.experimental.pallas import tpu as pltpu
from jax.sharding import PartitionSpec as P

CHUNKS = 2
UNROLL = 16
MESH_ID = pl.DeviceIdType.MESH


def link_slots(rows_ref, cols_ref, counts_ref, prev_ref, last_ref, *, slots, row_tiles, col_tiles):
    for side, (keys, size) in enumerate(((rows_ref, row_tiles), (cols_ref, col_tiles))):
        for k in range(size):
            last_ref[side, k] = slots
        for s in range(slots):
            key = keys[0, s]
            used = s < counts_ref[0, 0]
            before = last_ref[side, key]
            prev_ref[side, s] = jnp.where(used, before, slots)
            last_ref[side, key] = jnp.where(used, s, before)


def filter_kernel(
    dims, x_ref, tiles_ref, rows_ref, cols_ref, prev_ref, last_ref, center_ref, width_ref,
    out_ref, *scratch,
):
    R, C, half, pt, slots, vec, size = dims
    vc = vec // CHUNKS
    it = iter(scratch)
    win = [[next(it) for _ in range(CHUNKS)] for _ in range(2)]
    seg = [[next(it) for _ in range(CHUNKS)] for _ in range(2)]
    row_out = [[next(it) for _ in range(CHUNKS)] for _ in range(2)]
    col_out = [[next(it) for _ in range(CHUNKS)] for _ in range(2)]
    row_in = [[next(it) for _ in range(CHUNKS)] for _ in range(2)]
    col_in = [[next(it) for _ in range(CHUNKS)] for _ in range(2)]
    back = [next(it) for _ in range(CHUNKS)]
    direct = [next(it) for _ in range(CHUNKS)]
    mid = [[next(it) for _ in range(CHUNKS)] for _ in range(2)]
    result = next(it)
    tiles, local = next(it), next(it)
    row_send, row_recv, col_send, col_recv = (next(it) for _ in range(4))

    r = lax.axis_index("row")
    c = lax.axis_index("col")

    row_offsets = sorted({b % R for b in range(1, half + 1)} | {-b % R for b in range(1, half + 1)})
    barrier = pltpu.get_barrier_semaphore()
    for off in row_offsets:
        pl.semaphore_signal(barrier, inc=1, device_id={"row": lax.rem(r + off, R)}, device_id_type=MESH_ID)
    for off in range(1, C):
        pl.semaphore_signal(barrier, inc=1, device_id={"col": lax.rem(c + off, C)}, device_id_type=MESH_ID)

    fetch = pltpu.make_async_copy(tiles_ref.at[0], tiles, local)
    fetch.start()
    for end, slot in ((0, 0), (C - 1, C - 2)):
        @pl.when(c == end)
        def _():
            for t in range(2):
                for h in range(CHUNKS):
                    col_in[t][h][slot] = jnp.zeros((pt, vc, size), jnp.bfloat16)
    for j in range(pt):
        block = x_ref[j * size:(j + 1) * size, :].astype(jnp.float32).T.astype(jnp.bfloat16)
        for h in range(CHUNKS):
            part = block[h * vc:(h + 1) * vc, :]
            win[0][h][j] = part
            seg[0][h][c * pt + j] = part
    for h in range(CHUNKS):
        back[h][slots] = jnp.zeros((vc, size), jnp.float32)
        direct[h][slots] = jnp.zeros((vc, size), jnp.float32)
    pl.semaphore_wait(barrier, len(row_offsets) + C - 1)

    def gather_copies(t, h):
        own = win[t][h].at[pl.ds(0, pt)]
        cols = [
            pltpu.make_async_remote_copy(
                src_ref=own, dst_ref=seg[t][h].at[pl.ds(c * pt, pt)],
                send_sem=col_send.at[t, h, 0, d], recv_sem=col_recv.at[t, h, 0, d],
                device_id={"col": lax.rem(c + d, C)}, device_id_type=MESH_ID)
            for d in range(1, C)
        ]
        rows = [
            pltpu.make_async_remote_copy(
                src_ref=own, dst_ref=win[t][h].at[pl.ds(b * pt, pt)],
                send_sem=row_send.at[t, h, 0, b], recv_sem=row_recv.at[t, h, 0, b],
                device_id={"row": lax.rem(r + R - b, R)}, device_id_type=MESH_ID)
            for b in range(1, half + 1)
        ]
        return cols, rows

    def row_returns(t, h):
        return [
            pltpu.make_async_remote_copy(
                src_ref=row_out[t][h].at[b - 1], dst_ref=row_in[t][h].at[b - 1],
                send_sem=row_send.at[t, h, 1, b], recv_sem=row_recv.at[t, h, 1, b],
                device_id={"row": lax.rem(r + b, R)}, device_id_type=MESH_ID)
            for b in range(1, half + 1)
        ]

    def col_returns(t, h):
        return [
            pltpu.make_async_remote_copy(
                src_ref=col_out[t][h].at[d - 1], dst_ref=col_in[t][h].at[d - 1],
                send_sem=col_send.at[t, h, 1, d], recv_sem=col_recv.at[t, h, 1, d],
                device_id={"col": lax.rem(c + d, C)}, device_id_type=MESH_ID)
            for d in range(1, C)
        ]

    started = []

    def not_far(d):
        if d == C - 1:
            return c != 0
        return c != C - 1 if d == 1 else None

    def near_far(d):
        cond = None
        if d == 2:
            cond = c == C - 2
        if d == C - 2:
            cond = c == 1 if cond is None else cond | (c == 1)
        return cond

    def when(cond, act):
        if cond is None:
            act()
        else:
            pl.when(cond)(act)

    def start_if(copy, cond):
        when(cond, copy.start)
        drains.append((copy, cond))

    drains = []

    def forward(t, h, end):
        view = seg[t][h].at[pl.ds(end * pt, pt)]
        slot = 1 if end else C - 1
        return pltpu.make_async_remote_copy(
            src_ref=view, dst_ref=view,
            send_sem=col_send.at[t, h, 2, 0], recv_sem=col_recv.at[t, h, 0, slot],
            device_id={"col": lax.rem(c + (C - 1 if end else 1), C)}, device_id_type=MESH_ID)

    def to_mid(t, h, d):
        return pltpu.make_async_remote_copy(
            src_ref=col_out[t][h].at[d - 1], dst_ref=mid[t][h],
            send_sem=col_send.at[t, h, 1, d], recv_sem=col_recv.at[t, h, 1, 0],
            device_id={"col": lax.rem(c + C - d, C)}, device_id_type=MESH_ID)

    def start_gather(t, h):
        cols, rows = gather_copies(t, h)
        for d in sorted(range(1, C), key=lambda d: -min(d, C - d)):
            start_if(cols[d - 1], not_far(d))
        return cols, start_all(rows)

    def col_sums(t, h, d, helped):
        piece = lax.rem(c + d, C)
        for j in range(pt):
            value = direct[h][last_ref[0, piece * pt + j]]
            if helped:
                value += mid[t][h][j].astype(jnp.float32)
            col_out[t][h][d - 1, j] = value.astype(jnp.bfloat16)

    def return_plain(t, h):
        copies = col_returns(t, h)
        for d in sorted(range(1, C), key=lambda d: min(d, C - d)):
            helped = near_far(d)
            plain = None if helped is None else jnp.logical_not(helped)
            when(plain, lambda: col_sums(t, h, d, False))
            straight = not_far(d)
            if straight is not None:
                start_if(to_mid(t, h, d), jnp.logical_not(straight))
            both = straight if plain is None else plain if straight is None else plain & straight
            start_if(copies[d - 1], both)
        return copies

    def return_helped(t, h):
        copies = col_returns(t, h)
        for d in range(1, C):
            helped = near_far(d)
            if helped is not None:
                def add():
                    to_mid(t, h, d).wait_recv()
                    col_sums(t, h, d, True)

                when(helped, add)
                start_if(copies[d - 1], helped)

    def start_all(copies):
        for copy in copies:
            copy.start()
        started.extend(copies)
        return copies

    def products(source, index_ref, side, sums, transposed):
        contract = (((1,), (0,)), ((), ())) if transposed else (((1,), (1,)), ((), ()))

        def one(s, carry):
            term = lax.dot_general(
                source[index_ref[0, s]], tiles[s], contract,
                preferred_element_type=jnp.float32)
            sums[s] = sums[prev_ref[side, s]] + term
            return carry

        lax.fori_loop(0, slots, one, 0, unroll=UNROLL)

    def compute(t, h, copies):
        cols, rows = copies
        for d in sorted(range(1, C), key=lambda d: -min(d, C - d)):
            cols[d - 1].wait_recv()
            if d == C - 2:
                start_if(forward(t, h, 0), c == C - 2)
            if d == 2:
                start_if(forward(t, h, C - 1), c == 1)
        if t == 0 and h == 0:
            fetch.wait()
        products(seg[t][h], rows_ref, 1, back[h], True)
        for b in range(1, half + 1):
            for j in range(pt):
                row_out[t][h][b - 1, j] = back[h][last_ref[1, b * pt + j]].astype(jnp.bfloat16)
        returns = start_all(row_returns(t, h))
        if h:
            return_helped(t, h - 1)
        for copy in rows:
            copy.wait_recv()
        products(win[t][h], cols_ref, 0, direct[h], False)
        return returns, return_plain(t, h)

    def applied(t, h, returns, j):
        total = back[h][last_ref[1, j]] + direct[h][last_ref[0, c * pt + j]]
        for b in range(half):
            total += row_in[t][h][b, j].astype(jnp.float32)
        for d in range(C - 1):
            total += col_in[t][h][d, j].astype(jnp.float32)
        return total

    shift = center_ref[0]
    width = width_ref[0]
    gathers = [None] * CHUNKS
    for h in range(CHUNKS):
        gathers[h] = start_gather(0, h)
    for t in range(2):
        returns = [compute(t, h, gathers[h]) for h in range(CHUNKS)]
        return_helped(t, CHUNKS - 1)
        for h in range(CHUNKS):
            for copy in returns[h][0]:
                copy.wait_recv()
            for d in range(1, C):
                taken = c != 0 if d == 1 else c != C - 1 if d == C - 1 else None
                when(taken, returns[h][1][d - 1].wait_recv)
            for j in range(pt):
                begin = win[0][h][j].astype(jnp.float32)
                if t == 0:
                    first = ((applied(t, h, returns, j) - shift * begin) / width).astype(jnp.bfloat16)
                    win[1][h][j] = first
                    seg[1][h][c * pt + j] = first
                else:
                    first = win[1][h][j].astype(jnp.float32)
                    value = 2.0 * (applied(t, h, returns, j) - shift * first) / width - begin
                    result[j, h * vc:(h + 1) * vc, :] = value
            if t == 0:
                gathers[h] = start_gather(1, h)
    for j in range(pt):
        out_ref[j * size:(j + 1) * size, :] = result[j].T.astype(jnp.bfloat16)
    for copy in started:
        copy.wait_send()
    for copy, cond in drains:
        when(cond, copy.wait_send)


def per_device(start_vectors, tiles, tile_rows, tile_cols, tile_counts, center, half_width):
    R = lax.axis_size("row")
    C = lax.axis_size("col")
    half = R // 2
    piece_rows, vec = start_vectors.shape
    size = tiles.shape[-1]
    slots = tiles.shape[1]
    pt = piece_rows // size
    vc = vec // CHUNKS
    row_tiles = pt * C
    col_tiles = pt * (half + 1)
    smem = pl.BlockSpec(memory_space=pltpu.SMEM)
    vmem = pl.BlockSpec(memory_space=pltpu.VMEM)
    prev, last = pl.pallas_call(
        functools.partial(link_slots, slots=slots, row_tiles=row_tiles, col_tiles=col_tiles),
        out_shape=(
            jax.ShapeDtypeStruct((2, slots), jnp.int32),
            jax.ShapeDtypeStruct((2, max(row_tiles, col_tiles)), jnp.int32),
        ),
        in_specs=[smem] * 3,
        out_specs=(smem, smem),
        name="link_slots",
    )(tile_rows, tile_cols, tile_counts)

    bf, f32 = jnp.bfloat16, jnp.float32

    def pair(shape, dtype):
        return [pltpu.VMEM(shape, dtype) for _ in range(2 * CHUNKS)]

    scratch = (
        pair((col_tiles, vc, size), bf)
        + pair((row_tiles, vc, size), bf)
        + pair((half, pt, vc, size), bf)
        + pair((C - 1, pt, vc, size), bf)
        + pair((half, pt, vc, size), bf)
        + pair((C - 1, pt, vc, size), bf)
        + [pltpu.VMEM((slots + 1, vc, size), f32) for _ in range(2 * CHUNKS)]
        + pair((pt, vc, size), bf)
        + [pltpu.VMEM((pt, vec, size), f32), pltpu.VMEM((slots, size, size), bf), pltpu.SemaphoreType.DMA]
        + [pltpu.SemaphoreType.DMA((2, CHUNKS, 2, half + 1))] * 2
        + [pltpu.SemaphoreType.DMA((2, CHUNKS, 3, C))] * 2
    )
    return pl.pallas_call(
        functools.partial(filter_kernel, (R, C, half, pt, slots, vec, size)),
        out_shape=jax.ShapeDtypeStruct((piece_rows, vec), bf),
        in_specs=[vmem, pl.BlockSpec(memory_space=pl.ANY), smem, smem, smem, smem, smem, smem],
        out_specs=vmem,
        scratch_shapes=scratch,
        compiler_params=pltpu.CompilerParams(
            collective_id=0, has_side_effects=True, vmem_limit_bytes=40 << 20),
        name="filter_steps",
    )(start_vectors, tiles, tile_rows, tile_cols, prev, last, center, half_width)


def solution(mesh):
    return jax.shard_map(
        per_device,
        mesh=mesh,
        in_specs=(
            P(("row", "col"), None),
            P("row", "col", None, None),
            P("row", "col"),
            P("row", "col"),
            P("row", "col"),
            P(),
            P(),
        ),
        out_specs=P(("row", "col"), None),
        check_vma=False,
    )
```

profile of v0, /device:TPU:0, one launch (start us, length us, event | category | flops | bytes accessed | tf_op | source)
XLA Modules:
  0.0 57.3 jit_solution(17426468510959127212)
XLA Ops:
  1.9 1.6 %link_slots.1 = (s32[2,32]{1,0:T(2,128)}, s32[2,20]{1,0:T(2,128)}) custom-call(s32[1,32]{1,0:T(1,128)} %rows_ref.3, s32[1,32]{1,0:T(1,128)} %cols_ref.3, s32[1,1]{1,0:T(1,128)S(6)} %copy.9.counts_ref), custom_call_target="tpu_custom_call" | custom-call | tf_op jit(solution)/shard_map/link_slots/pallas_call | solution.py:287
  3.6 0.0 copy-start.3
  3.6 0.0 copy-start.5
  3.6 0.0 copy-start.2
  3.6 0.0 copy-start.4
  3.6 0.6 %copy-done.3 = s32[2,20]{1,0:T(2,128)S(1)} copy-done((s32[2,20]{1,0:T(2,128)S(1)}, s32[2,20]{1,0:T(2,128)}, u32[]{:S(2)}) %copy-start.3) | copy-done | bytes 184
  4.2 0.0 copy-done.5
  4.2 0.0 copy-done.2
  4.3 0.0 copy-done.4
  4.3 0.0 copy-start
  4.3 1.2 %copy-done = bf16[1,32,128,128]{3,2,1,0:T(8,128)(2,1)S(1)} copy-done((bf16[1,32,128,128]{3,2,1,0:T(8,128)(2,1)S(1)}, bf16[1,32,128,128]{3,2,1,0:T(8,128)(2,1)}, u32[]{:S(2)}) %copy-start) | copy-done | bytes 1048600
  5.5 0.0 copy-start.1
  5.5 0.9 %copy-done.1 = bf16[512,128]{1,0:T(8,128)(2,1)S(1)} copy-done((bf16[512,128]{1,0:T(8,128)(2,1)S(1)}, bf16[512,128]{1,0:T(8,128)(2,1)}, u32[]{:S(2)}) %copy-start.1) | copy-done | bytes 131096
  6.4 50.3 %filter_steps.1 = bf16[512,128]{1,0:T(8,128)(2,1)S(1)} custom-call(bf16[512,128]{1,0:T(8,128)(2,1)S(1)} %copy-done.1, bf16[1,32,128,128]{3,2,1,0:T(8,128)(2,1)S(1)} %copy-done, s32[1,32]{1,0:T(1,128)S(1)} %copy-done.4, s32[1,32]{1,0:T(1,128)S(1)} %copy-done.5, s32[2,32]{1,0:T(2,128)S(1)} %copy-done.2, s32[2,20]{1,0:T(2,128)S(1)} %copy-done.3, ...), custom_call_target="tpu_custom_call" | custom-call | tf_op jit(solution)/shard_map/filter_steps/pallas_call | solution.py:316
  56.7 0.7 %copy.12 = bf16[512,128]{1,0:T(8,128)(2,1)} copy(bf16[512,128]{1,0:T(8,128)(2,1)S(1)} %filter_steps.1) | data formatting | bytes 262144
Async XLA Ops:
  3.6 0.7 %copy-start.3 = (s32[2,20]{1,0:T(2,128)S(1)}, s32[2,20]{1,0:T(2,128)}, u32[]{:S(2)}) copy-start(s32[2,20]{1,0:T(2,128)} %get-tuple-element.8.last_ref) | copy-start | bytes 484
  3.6 0.7 %copy-start.5 = (s32[1,32]{1,0:T(1,128)S(1)}, s32[1,32]{1,0:T(1,128)}, u32[]{:S(2)}) copy-start(s32[1,32]{1,0:T(1,128)} %cols_ref.3) | copy-start | bytes 388
  3.6 0.7 %copy-start.2 = (s32[2,32]{1,0:T(2,128)S(1)}, s32[2,32]{1,0:T(2,128)}, u32[]{:S(2)}) copy-start(s32[2,32]{1,0:T(2,128)} %get-tuple-element.7.prev_ref) | copy-start | bytes 772
  3.6 0.7 %copy-start.4 = (s32[1,32]{1,0:T(1,128)S(1)}, s32[1,32]{1,0:T(1,128)}, u32[]{:S(2)}) copy-start(s32[1,32]{1,0:T(1,128)} %rows_ref.3) | copy-start | bytes 388
  4.3 1.2 %copy-start = (bf16[1,32,128,128]{3,2,1,0:T(8,128)(2,1)S(1)}, bf16[1,32,128,128]{3,2,1,0:T(8,128)(2,1)}, u32[]{:S(2)}) copy-start(bf16[1,32,128,128]{3,2,1,0:T(8,128)(2,1)} %tiles_ref.1) | copy-start | bytes 3145732
  5.5 0.9 %copy-start.1 = (bf16[512,128]{1,0:T(8,128)(2,1)S(1)}, bf16[512,128]{1,0:T(8,128)(2,1)}, u32[]{:S(2)}) copy-start(bf16[512,128]{1,0:T(8,128)(2,1)} %x_ref.1) | copy-start | bytes 393220
where the time goes:
time: 57.6 us; the launch traced here: 57.3 us
  Pallas kernels  51.9 us (90%)
  local copies, waits for them, and re-layouts  3.46 us (6%)
  between operations  1.99 us (3%)
    pallas_call x1, Pallas kernels, per_device(): pl.pallas_call(functools.partial(filter_kernel, (R, C, half, pt, slots, v...  50.3 us
    unnamed x13, local copies, waits for them, and re-layouts  3.46 us
    pallas_call x1, Pallas kernels, per_device(): pl.pallas_call(functools.partial(link_slots, slots=slots, row_tiles=row_t...  1.61 us

commit v1 on v0

v1 whole, which is shorter than its diff:
```python
import functools

import jax
import jax.numpy as jnp
from jax import lax
from jax.experimental import pallas as pl
from jax.experimental.pallas import tpu as pltpu
from jax.sharding import PartitionSpec as P

CHUNKS = 2
UNROLL = 16
MESH_ID = pl.DeviceIdType.MESH
GATHER_TREES = (("tail", "tail"), ("tail", "tail"))
REDUCE_TREES = (("tail", "tail"), ("tail", "tail"))
ORDER = ()


def parent(kind, length, dist):
    if kind == "chain":
        return dist - 1
    if kind == "tail":
        return dist - 1 if dist == length and length >= 2 else 0
    if kind == "tail3":
        return dist - 1 if dist == length and length >= 3 else 0
    return 0


def side(c, sgn, C):
    return c if sgn > 0 else C - 1 - c


def default_order(K, C):
    far = range(2, C - 1)
    order = [("Gs", 0, h) for h in range(K)]
    for t in range(2):
        for h in range(K):
            order += [("XF", t, h), ("GF1", t, h), ("D", t, h)]
        for h in range(K):
            order += [("GF%d" % d, t, h) for d in far]
            order += [("RM%d" % d, t, h) for d in reversed(far)] + [("RM1", t, h)]
            order += [("B", t, h), ("RX", t, h)]
        for h in range(K):
            order.append(("E", t, h))
            if t == 0:
                order.append(("Gs", 1, h))
    return order


def full_order(K, C, hq):
    base = [(s[:-2], int(s[-2]), int(s[-1])) for s in ORDER] or default_order(K, C)
    known = set(base)
    order = []
    for name, t, h in base:
        if name == "B":
            order += [("GF%d" % d, t, h) for d in range(1, C - 1) if ("GF%d" % d, t, h) not in known]
        if name == "E":
            order += [("RM%d" % d, t, h) for d in range(C - 2, 0, -1) if ("RM%d" % d, t, h) not in known]
        if name == "XF":
            order += [("XF%d" % d, t, h) for d in range(1, hq + 1)]
        elif name == "RX":
            order += [("RX%d" % d, t, h) for d in range(hq, 0, -1)]
        else:
            if name == "D":
                order += [("XF%d" % d, t, h) for d in range(1, hq + 1)
                          if ("XF%d" % d, t, h) not in known and ("XF", t, h) not in known]
            if name == "E":
                order += [("RX%d" % d, t, h) for d in range(hq, 0, -1)
                          if ("RX%d" % d, t, h) not in known and ("RX", t, h) not in known]
            order.append((name, t, h))
    return order


def filter_kernel(
    dims, x_ref, tiles_ref, rows_ref, cols_ref, counts_ref, center_ref, width_ref, out_ref, *scratch,
):
    R, C, half, pt, slots, vec, size = dims
    K = CHUNKS
    vc = vec // K
    hq = half // 2
    ways = 2 * (C - 1)
    it = iter(scratch)

    def pair():
        return [[next(it) for _ in range(K)] for _ in range(2)]

    win, seg, pair_out, row_out, pair_in, row_in = pair(), pair(), pair(), pair(), pair(), pair()
    col_out, col_fin, col_mid = pair(), pair(), pair()
    back = [next(it) for _ in range(K)]
    direct = [next(it) for _ in range(K)]
    x_in, result, tiles, keys, table = next(it), next(it), next(it), next(it), next(it)
    row_of, col_of, links = next(it), next(it), next(it)
    local, row_send, row_recv, col_send, col_recv = next(it), next(it), next(it), next(it), next(it)

    r = lax.axis_index("row")
    c = lax.axis_index("col")
    k = lax.rem(r, 2)
    partner = r + 1 - 2 * k

    def among(test):
        members = [n for n in range(C) if test(n)]
        if len(members) in (0, C):
            return bool(members)
        cond = None
        for lo in members:
            if lo - 1 in members:
                continue
            hi = lo
            while hi + 1 in members:
                hi += 1
            one = c == lo if lo == hi else c <= hi if lo == 0 else c >= lo if hi == C - 1 else (c >= lo) & (c <= hi)
            cond = one if cond is None else cond | one
        return cond

    def when(cond, act):
        if cond is True:
            act()
        elif cond is not False:
            pl.when(cond)(act)

    barrier = pltpu.get_barrier_semaphore()
    row_peers = sorted({d % R for d in range(2, half + 1, 2)} | {-d % R for d in range(2, half + 1, 2)})
    for off in row_peers:
        pl.semaphore_signal(barrier, inc=1, device_id={"row": lax.rem(r + off, R)}, device_id_type=MESH_ID)
    pl.semaphore_signal(barrier, inc=1, device_id={"row": partner}, device_id_type=MESH_ID)
    for off in range(1, C):
        pl.semaphore_signal(barrier, inc=1, device_id={"col": lax.rem(c + off, C)}, device_id_type=MESH_ID)

    load_x = pltpu.make_async_copy(x_ref, x_in, local.at[0])
    load_x.start()
    smem_loads = [
        pltpu.make_async_copy(rows_ref, row_of, local.at[1]),
        pltpu.make_async_copy(cols_ref, col_of, local.at[2]),
    ]
    key_loads = [
        pltpu.make_async_copy(rows_ref, keys.at[0], local.at[3]),
        pltpu.make_async_copy(cols_ref, keys.at[1], local.at[4]),
    ]
    for copy in key_loads + smem_loads:
        copy.start()
    fetch = pltpu.make_async_copy(tiles_ref.at[0], tiles, local.at[5])
    fetch.start()

    def way(sgn, d):
        return 2 * (d - 1) + (0 if sgn > 0 else 1)

    def tiles_at(ref, slot):
        return ref.at[pl.ds(slot * pt, pt)]

    sgns = (1, -1)
    dists = range(1, C)
    final = {}
    for t in range(2):
        for h in range(K):
            for sgn in sgns:
                for d in dists:
                    def test(n, t=t, h=h, sgn=sgn, d=d):
                        return d <= side(n, sgn, C) and parent(REDUCE_TREES[t][h], side(n, sgn, C), d) == 0
                    cond = among(test)
                    final[t, h, sgn, d] = cond
                    if cond is not True and cond is not False:
                        def clear(t=t, h=h, sgn=sgn, d=d):
                            tiles_at(col_fin[t][h], way(sgn, d))[...] = jnp.zeros((pt, vc, size), jnp.bfloat16)
                        pl.when(jnp.logical_not(cond))(clear)
            tiles_at(pair_in[t][h], hq)[...] = jnp.zeros((pt, vc, size), jnp.bfloat16)
    for h in range(K):
        back[h][slots] = jnp.zeros((vc, size), jnp.float32)
        direct[h][slots] = jnp.zeros((vc, size), jnp.float32)

    load_x.wait()
    for j in range(pt):
        block = x_in[j * size:(j + 1) * size, :].astype(jnp.float32).T.astype(jnp.bfloat16)
        for h in range(K):
            part = block[h * vc:(h + 1) * vc, :]
            win[0][h][j] = part
            seg[0][h][c * pt + j] = part
    pl.semaphore_wait(barrier, len(row_peers) + 1 + C - 1)

    drains = []

    def start(copy, cond=True):
        when(cond, copy.start)
        drains.append((copy, cond))

    def to_row(src, dst, t, h, send, recv, row):
        return pltpu.make_async_remote_copy(
            src_ref=src, dst_ref=dst, send_sem=row_send.at[t, h, send], recv_sem=row_recv.at[t, h, recv],
            device_id={"row": row}, device_id_type=MESH_ID)

    def to_col(src, dst, t, h, send, recv, col):
        return pltpu.make_async_remote_copy(
            src_ref=src, dst_ref=dst, send_sem=col_send.at[t, h, send], recv_sem=col_recv.at[t, h, recv],
            device_id={"col": col}, device_id_type=MESH_ID)

    def up(d):
        return lax.rem(r + d, R)

    def piece_copy(t, h, d):
        return to_row(tiles_at(win[t][h], 0), tiles_at(win[t][h], 2 * d), t, h, 2 * d, 2 * d, up(R - 2 * d))

    def partner_copy(t, h, d):
        slot = 2 * d - 1 + 2 * k
        return to_row(tiles_at(win[t][h], 2 * d), tiles_at(win[t][h], slot), t, h, slot, slot, partner)

    def piece_arrival(t, h, b):
        view = tiles_at(win[t][h], b)
        return to_row(view, view, t, h, b, b, partner)

    def pair_copy(t, h, j):
        at = half + j
        return to_row(
            tiles_at(pair_out[t][h], j - 1), tiles_at(pair_in[t][h], j - 1), t, h, at, at, partner)

    def row_copy(t, h, d):
        at = half + hq + d
        return to_row(
            tiles_at(row_out[t][h], d - 1), tiles_at(row_in[t][h], d - 1), t, h, at, at, up(2 * d))

    def col_piece(t, h, sgn, d, hop):
        p = c - sgn * d
        view = tiles_at(seg[t][h], p)
        src = view if d else tiles_at(win[t][h], 0)
        send = way(sgn, hop) if d == 0 else ways + way(sgn, d)
        return to_col(src, view, t, h, send, p, c + sgn * hop)

    def col_arrival(t, h, sgn, d):
        p = c - sgn * d
        view = tiles_at(seg[t][h], p)
        return to_col(view, view, t, h, 0, p, p)

    def gather_child(t, h, sgn, d, hop):
        kind = GATHER_TREES[t][h]

        def test(n):
            root = n - sgn * d
            if not 0 <= root < C or not 0 <= n + sgn * hop < C:
                return False
            length = side(C - 1 - root, sgn, C)
            return parent(kind, length, d + hop) == d
        return among(test)

    def start_gather(t, h):
        for d in range(hq, 0, -1):
            start(piece_copy(t, h, d))
        start(partner_copy(t, h, 0), k == 1)
        for hop in reversed(dists):
            for sgn in sgns:
                cond = gather_child(t, h, sgn, 0, hop)
                if cond is not False:
                    start(col_piece(t, h, sgn, 0, hop), cond)

    def forward_row(t, h, d):
        piece_arrival(t, h, 2 * d).wait_recv()
        start(partner_copy(t, h, d), True if d < hq else k == 0)

    def forward_col(t, h, d):
        for sgn in sgns:
            cond = gather_child(t, h, sgn, d, 1)
            if cond is False:
                continue
            when(cond, col_arrival(t, h, sgn, d).wait_recv)
            start(col_piece(t, h, sgn, d, 1), cond)

    def products(source, index_ref, side_row, sums, transposed):
        contract = (((1,), (0,)), ((), ())) if transposed else (((1,), (1,)), ((), ()))

        def one(s, carry):
            term = lax.dot_general(
                source[index_ref[0, s]], tiles[s], contract,
                preferred_element_type=jnp.float32)
            sums[s] = sums[links[side_row, s]] + term
            return carry

        lax.fori_loop(0, slots, one, 0, unroll=UNROLL)

    def reduce_groups(t, h, sgn, d):
        kind = REDUCE_TREES[t][h]

        def of(n):
            dest = n + sgn * d
            if not 0 <= dest < C:
                return None
            length = side(dest, sgn, C)
            return parent(kind, length, d), d < length and parent(kind, length, d + 1) == d
        found = sorted({of(n) for n in range(C)} - {None})
        return [(left, helped, among(lambda n: of(n) == (left, helped))) for left, helped in found]

    def reduce_copy(t, h, sgn, d, left):
        w = way(sgn, d)
        src = tiles_at(col_out[t][h], w)
        if left == 0:
            return to_col(src, tiles_at(col_fin[t][h], w), t, h, 2 * ways + w, C + w, c + sgn * d)
        m = way(sgn, left)
        return to_col(src, tiles_at(col_mid[t][h], m), t, h, 2 * ways + w, C + ways + m, c + sgn * (d - left))

    def mid_arrival(t, h, sgn, d):
        m = way(sgn, d)
        view = tiles_at(col_mid[t][h], m)
        return to_col(view, view, t, h, 0, C + ways + m, c)

    def fin_arrival(t, h, sgn, d):
        w = way(sgn, d)
        view = tiles_at(col_fin[t][h], w)
        return to_col(view, view, t, h, 0, C + w, c)

    def pass_on(t, h, d, want):
        for sgn in sgns:
            for left, helped, cond in reduce_groups(t, h, sgn, d):
                if helped != want:
                    continue

                def act(sgn=sgn, helped=helped):
                    if helped:
                        mid_arrival(t, h, sgn, d).wait_recv()
                    dest = c + sgn * d
                    for j in range(pt):
                        value = direct[h][links[2, dest * pt + j]]
                        if helped:
                            value += col_mid[t][h][way(sgn, d) * pt + j].astype(jnp.float32)
                        col_out[t][h][way(sgn, d) * pt + j] = value.astype(jnp.bfloat16)
                when(cond, act)
                start(reduce_copy(t, h, sgn, d, left), cond)

    def do_direct(t, h):
        for b in range(1, half + 1, 2):
            piece_arrival(t, h, b).wait_recv()
        products(win[t][h], col_of, 0, direct[h], False)
        for d in reversed(dists):
            pass_on(t, h, d, False)

    def do_back(t, h):
        for sgn in sgns:
            for d in dists:
                def test(n, sgn=sgn, d=d):
                    return d <= side(n, sgn, C)

                def sent(n, sgn=sgn, d=d):
                    root, nxt = n - sgn * d, n + sgn
                    return 0 <= nxt < C and parent(GATHER_TREES[t][h], side(C - 1 - root, sgn, C), d + 1) == d
                cond = among(lambda n: test(n) and not sent(n))
                if cond is not False:
                    when(cond, col_arrival(t, h, sgn, d).wait_recv)
        products(seg[t][h], row_of, 1, back[h], True)
        for i in range(1, hq + 1):
            for j in range(pt):
                pair_out[t][h][(i - 1) * pt + j] = back[h][links[3, (2 * i - 1) * pt + j]].astype(jnp.bfloat16)
            start(pair_copy(t, h, i))

    def return_row(t, h, d):
        arrival = pair_copy(t, h, d)
        if d < hq:
            slot = d - 1 + k
            view = tiles_at(pair_in[t][h], slot)
            to_row(view, view, t, h, half + 1 + slot, half + 1 + slot, partner).wait_recv()
        else:
            slot = d - 1 + k
            pl.when(k == 0)(arrival.wait_recv)
        for j in range(pt):
            value = back[h][links[3, 2 * d * pt + j]] + pair_in[t][h][slot * pt + j].astype(jnp.float32)
            row_out[t][h][(d - 1) * pt + j] = value.astype(jnp.bfloat16)
        start(row_copy(t, h, d))

    shift = center_ref[0]
    width = width_ref[0]

    def finish(t, h):
        pl.when(k == 1)(pair_copy(t, h, 1).wait_recv)
        for d in range(1, hq + 1):
            row_copy(t, h, d).wait_recv()
        for sgn in sgns:
            for d in dists:
                cond = final[t, h, sgn, d]
                if cond is not False:
                    when(cond, fin_arrival(t, h, sgn, d).wait_recv)
        slot = jnp.where(k == 1, 0, hq)
        for j in range(pt):
            total = back[h][links[3, j]] + direct[h][links[2, c * pt + j]]
            total += pair_in[t][h][slot * pt + j].astype(jnp.float32)
            for d in range(hq):
                total += row_in[t][h][d * pt + j].astype(jnp.float32)
            for sgn in sgns:
                for d in dists:
                    if final[t, h, sgn, d] is not False:
                        total += col_fin[t][h][way(sgn, d) * pt + j].astype(jnp.float32)
            begin = win[0][h][j].astype(jnp.float32)
            if t == 0:
                first = ((total - shift * begin) / width).astype(jnp.bfloat16)
                win[1][h][j] = first
                seg[1][h][c * pt + j] = first
            else:
                first = win[1][h][j].astype(jnp.float32)
                result[j, h * vc:(h + 1) * vc, :] = 2.0 * (total - shift * first) / width - begin

    def link_slots():
        for copy in key_loads:
            copy.wait()
        count = counts_ref[0, 0]
        sub = lax.broadcasted_iota(jnp.int32, (slots, slots), 0)
        lane = lax.broadcasted_iota(jnp.int32, (slots, slots), 1)
        sub_w = lax.broadcasted_iota(jnp.int32, (slots, size), 0)
        lane_w = lax.broadcasted_iota(jnp.int32, (slots, size), 1)
        for i in range(2):
            key = jnp.broadcast_to(keys[i], (slots, slots))
            column = jnp.max(jnp.where(lane == sub, key, -1), axis=1, keepdims=True)
            same = (column == key) & (sub < lane) & (sub < count)
            before = jnp.max(jnp.where(same, sub, -1), axis=0, keepdims=True)
            table[i:i + 1, 0:slots] = jnp.where(before < 0, slots, before)
            hit = (column == lane_w) & (sub_w < count)
            last = jnp.max(jnp.where(hit, sub_w, -1), axis=0, keepdims=True)
            table[2 + i:3 + i, :] = jnp.where(last < 0, slots, last)
        publish = pltpu.make_async_copy(table, links, local.at[6])
        publish.start()
        for copy in smem_loads:
            copy.wait()
        publish.wait()

    waited = False
    for name, t, h in full_order(K, C, hq):
        if name in ("D", "B") and not waited:
            fetch.wait()
            waited = True
        if name == "Gs":
            start_gather(t, h)
            if (t, h) == (0, K - 1):
                link_slots()
        elif name == "D":
            do_direct(t, h)
        elif name == "B":
            do_back(t, h)
        elif name == "E":
            finish(t, h)
        else:
            act = {"XF": forward_row, "GF": forward_col, "RX": return_row}.get(name[:2])
            if act is not None:
                act(t, h, int(name[2:]))
            else:
                pass_on(t, h, int(name[2:]), True)
    for j in range(pt):
        out_ref[j * size:(j + 1) * size, :] = result[j].T.astype(jnp.bfloat16)
    for copy, cond in drains:
        when(cond, copy.wait_send)


def per_device(start_vectors, tiles, tile_rows, tile_cols, tile_counts, center, half_width):
    R = lax.axis_size("row")
    C = lax.axis_size("col")
    half = R // 2
    hq = half // 2
    piece_rows, vec = start_vectors.shape
    size = tiles.shape[-1]
    slots = tiles.shape[1]
    pt = piece_rows // size
    vc = vec // CHUNKS
    ways = 2 * (C - 1)
    smem = pl.BlockSpec(memory_space=pltpu.SMEM)
    vmem = pl.BlockSpec(memory_space=pltpu.VMEM)
    anywhere = pl.BlockSpec(memory_space=pl.ANY)
    bf, f32, i32 = jnp.bfloat16, jnp.float32, jnp.int32

    def pair(count):
        return [pltpu.VMEM((count * pt, vc, size), bf) for _ in range(2 * CHUNKS)]

    scratch = (
        pair(half + 1) + pair(C) + pair(hq) + pair(hq) + pair(hq + 1) + pair(hq)
        + pair(ways) + pair(ways) + pair(ways)
        + [pltpu.VMEM((slots + 1, vc, size), f32) for _ in range(2 * CHUNKS)]
        + [
            pltpu.VMEM((piece_rows, vec), bf), pltpu.VMEM((pt, vec, size), f32),
            pltpu.VMEM((slots, size, size), bf),
            pltpu.VMEM((2, 1, slots), i32), pltpu.VMEM((4, size), i32),
            pltpu.SMEM((1, slots), i32), pltpu.SMEM((1, slots), i32), pltpu.SMEM((4, size), i32),
            pltpu.SemaphoreType.DMA((7,)),
        ]
        + [pltpu.SemaphoreType.DMA((2, CHUNKS, half + 2 * hq + 1))] * 2
        + [pltpu.SemaphoreType.DMA((2, CHUNKS, 3 * ways))]
        + [pltpu.SemaphoreType.DMA((2, CHUNKS, C + 2 * ways))]
    )
    return pl.pallas_call(
        functools.partial(filter_kernel, (R, C, half, pt, slots, vec, size)),
        out_shape=jax.ShapeDtypeStruct((piece_rows, vec), bf),
        in_specs=[anywhere] * 4 + [smem] * 3,
        out_specs=vmem,
        scratch_shapes=scratch,
        compiler_params=pltpu.CompilerParams(
            collective_id=0, has_side_effects=True, vmem_limit_bytes=VMEM_LIMIT),
        name="filter_steps",
    )(start_vectors, tiles, tile_rows, tile_cols, tile_counts, center, half_width)


VMEM_LIMIT = 66_800_000


def solution(mesh):
    return jax.shard_map(
        per_device,
        mesh=mesh,
        in_specs=(
            P(("row", "col"), None),
            P("row", "col", None, None),
            P("row", "col"),
            P("row", "col"),
            P("row", "col"),
            P(),
            P(),
        ),
        out_specs=P(("row", "col"), None),
        check_vma=False,
    )
```

time: 57.6 us -> 57.7 us (level)
  Pallas kernels: 51.9 us -> 54 us
  local copies, waits for them, and re-layouts: 3.46 us -> 1.57 us
    pallas_call x1, Pallas kernels: 50.3 us -> 54 us  [per_device(): pl.pallas_call(functools.partial(filter_kernel, (R, C, half, pt, slots, v...]
    unnamed x13 -> x1, local copies, waits for them, and re-layouts: 3.46 us -> 1.57 us
    pallas_call x1 -> x0, Pallas kernels: 1.61 us -> none  [per_device(): pl.pallas_call(functools.partial(link_slots, slots=slots, row_tiles=row_t...]
where the time goes in v1:
time: 57.7 us; the launch traced here: 57.5 us
  Pallas kernels  54 us (94%)
  between operations  1.95 us (3%)
  local copies, waits for them, and re-layouts  1.57 us (3%)
    pallas_call x1, Pallas kernels, per_device(): pl.pallas_call(functools.partial(filter_kernel, (R, C, half, pt, slots, v...  54 us
    unnamed x1, local copies, waits for them, and re-layouts  1.57 us

profile of v1, /device:TPU:0, one launch (start us, length us, event | category | flops | bytes accessed | tf_op | source)
XLA Modules:
  0.0 57.5 jit_solution(11827666643692512438)
XLA Ops:
  1.9 54.0 %filter_steps.1 = bf16[512,128]{1,0:T(8,128)(2,1)} custom-call(bf16[512,128]{1,0:T(8,128)(2,1)} %x_ref.1, bf16[1,32,128,128]{3,2,1,0:T(8,128)(2,1)} %tiles_ref.1, s32[1,32]{1,0:T(1,128)} %rows_ref.1, s32[1,32]{1,0:T(1,128)} %cols_ref.1, s32[1,1]{1,0:T(1,128)S(6)} %copy.9.counts_ref, f32[1]{0:T(128)S(6)} %copy.10.center_ref, f32[1]{0:T(128)S(6)} %copy.11.width_ref), custom_call_target="tpu_custom_call" | custom-call | tf_op jit(solution)/shard_map/filter_steps/pallas_call | solution.py:477
  55.9 1.6 %copy.12 = bf16[512,128]{1,0:T(8,128)(2,1)} copy(bf16[512,128]{1,0:T(8,128)(2,1)} %filter_steps.1) | data formatting | bytes 262144

commit v2 on v1

--- a/solution.py
+++ b/solution.py
@@ -1,3 +1,4 @@
+import contextlib
 import functools
 
 import jax
@@ -10,9 +11,17 @@
 CHUNKS = 2
 UNROLL = 16
 MESH_ID = pl.DeviceIdType.MESH
-GATHER_TREES = (("tail", "tail"), ("tail", "tail"))
+GATHER_TREES = (("tail3", "tail3"), ("tail3", "tail"))
 REDUCE_TREES = (("tail", "tail"), ("tail", "tail"))
-ORDER = ()
+ORDER = (
+    "Gs00", "GF200", "XF100", "GF100", "GF101", "Gs01", "XF200", "D00",
+    "XF101", "B00", "GF201", "RX200", "RX100", "XF201", "D01", "RM100",
+    "B01", "RX201", "RM200", "RM201", "RX101", "RM101", "E00", "Gs10",
+    "E01", "XF110", "Gs11", "XF210", "GF210", "D10", "GF110", "GF211",
+    "XF111", "B10", "XF211", "GF111", "RX110", "RM210", "D11", "RX210",
+    "B11", "RM110", "RM211", "RX211", "RX111", "RM111", "E10", "E11",
+)
+SCOPE = contextlib.nullcontext
 
 
 def parent(kind, length, dist):
@@ -71,7 +80,7 @@
 
 
 def filter_kernel(
-    dims, x_ref, tiles_ref, rows_ref, cols_ref, counts_ref, center_ref, width_ref, out_ref, *scratch,
+    dims, x_ref, tiles_ref, row_of, col_of, counts_ref, center_ref, width_ref, out_ref, *scratch,
 ):
     R, C, half, pt, slots, vec, size = dims
     K = CHUNKS
@@ -87,8 +96,7 @@
     col_out, col_fin, col_mid = pair(), pair(), pair()
     back = [next(it) for _ in range(K)]
     direct = [next(it) for _ in range(K)]
-    x_in, result, tiles, keys, table = next(it), next(it), next(it), next(it), next(it)
-    row_of, col_of, links = next(it), next(it), next(it)
+    x_in, result, tiles, table, links = next(it), next(it), next(it), next(it), next(it)
     local, row_send, row_recv, col_send, col_recv = next(it), next(it), next(it), next(it), next(it)
 
     r = lax.axis_index("row")
@@ -127,17 +135,7 @@
 
     load_x = pltpu.make_async_copy(x_ref, x_in, local.at[0])
     load_x.start()
-    smem_loads = [
-        pltpu.make_async_copy(rows_ref, row_of, local.at[1]),
-        pltpu.make_async_copy(cols_ref, col_of, local.at[2]),
-    ]
-    key_loads = [
-        pltpu.make_async_copy(rows_ref, keys.at[0], local.at[3]),
-        pltpu.make_async_copy(cols_ref, keys.at[1], local.at[4]),
-    ]
-    for copy in key_loads + smem_loads:
-        copy.start()
-    fetch = pltpu.make_async_copy(tiles_ref.at[0], tiles, local.at[5])
+    fetch = pltpu.make_async_copy(tiles_ref.at[0], tiles, local.at[1])
     fetch.start()
 
     def way(sgn, d):
@@ -166,14 +164,16 @@
         back[h][slots] = jnp.zeros((vc, size), jnp.float32)
         direct[h][slots] = jnp.zeros((vc, size), jnp.float32)
 
-    load_x.wait()
+    with SCOPE("loadx"):
+        load_x.wait()
     for j in range(pt):
         block = x_in[j * size:(j + 1) * size, :].astype(jnp.float32).T.astype(jnp.bfloat16)
         for h in range(K):
             part = block[h * vc:(h + 1) * vc, :]
             win[0][h][j] = part
             seg[0][h][c * pt + j] = part
-    pl.semaphore_wait(barrier, len(row_peers) + 1 + C - 1)
+    with SCOPE("greet"):
+        pl.semaphore_wait(barrier, len(row_peers) + 1 + C - 1)
 
     drains = []
 
@@ -391,53 +391,57 @@
                 result[j, h * vc:(h + 1) * vc, :] = 2.0 * (total - shift * first) / width - begin
 
     def link_slots():
-        for copy in key_loads:
-            copy.wait()
         count = counts_ref[0, 0]
-        sub = lax.broadcasted_iota(jnp.int32, (slots, slots), 0)
-        lane = lax.broadcasted_iota(jnp.int32, (slots, slots), 1)
-        sub_w = lax.broadcasted_iota(jnp.int32, (slots, size), 0)
-        lane_w = lax.broadcasted_iota(jnp.int32, (slots, size), 1)
-        for i in range(2):
-            key = jnp.broadcast_to(keys[i], (slots, slots))
-            column = jnp.max(jnp.where(lane == sub, key, -1), axis=1, keepdims=True)
-            same = (column == key) & (sub < lane) & (sub < count)
+        sub = lax.broadcasted_iota(jnp.int32, (slots, size), 0)
+        lane = lax.broadcasted_iota(jnp.int32, (slots, size), 1)
+        for i, keys in enumerate((row_of, col_of)):
+            key = jnp.full((slots, size), -1, jnp.int32)
+            column = key
+            for s in range(slots):
+                one = keys[0, s]
+                key = jnp.where(lane == s, one, key)
+                column = jnp.where(sub == s, one, column)
+            used = sub < count
+            same = (column == key) & (sub < lane) & used
             before = jnp.max(jnp.where(same, sub, -1), axis=0, keepdims=True)
-            table[i:i + 1, 0:slots] = jnp.where(before < 0, slots, before)
-            hit = (column == lane_w) & (sub_w < count)
-            last = jnp.max(jnp.where(hit, sub_w, -1), axis=0, keepdims=True)
+            table[i:i + 1, :] = jnp.where(before < 0, slots, before)
+            last = jnp.max(jnp.where((column == lane) & used, sub, -1), axis=0, keepdims=True)
             table[2 + i:3 + i, :] = jnp.where(last < 0, slots, last)
-        publish = pltpu.make_async_copy(table, links, local.at[6])
+        publish = pltpu.make_async_copy(table, links, local.at[2])
         publish.start()
-        for copy in smem_loads:
-            copy.wait()
         publish.wait()
 
-    waited = False
-    for name, t, h in full_order(K, C, hq):
-        if name in ("D", "B") and not waited:
-            fetch.wait()
-            waited = True
+    def run(name, t, h):
         if name == "Gs":
             start_gather(t, h)
-            if (t, h) == (0, K - 1):
-                link_slots()
         elif name == "D":
             do_direct(t, h)
         elif name == "B":
             do_back(t, h)
         elif name == "E":
             finish(t, h)
+        elif name[:2] == "RM":
+            pass_on(t, h, int(name[2:]), True)
         else:
-            act = {"XF": forward_row, "GF": forward_col, "RX": return_row}.get(name[:2])
-            if act is not None:
-                act(t, h, int(name[2:]))
-            else:
-                pass_on(t, h, int(name[2:]), True)
-    for j in range(pt):
-        out_ref[j * size:(j + 1) * size, :] = result[j].T.astype(jnp.bfloat16)
-    for copy, cond in drains:
-        when(cond, copy.wait_send)
+            {"XF": forward_row, "GF": forward_col, "RX": return_row}[name[:2]](t, h, int(name[2:]))
+
+    linked = False
+    for name, t, h in full_order(K, C, hq):
+        if not linked and name in ("D", "B"):
+            with SCOPE("link"):
+                link_slots()
+            linked = True
+        if name in ("D", "B") and fetch is not None:
+            fetch.wait()
+            fetch = None
+        with SCOPE("%s_%d%d" % (name, t, h)):
+            run(name, t, h)
+    with SCOPE("out"):
+        for j in range(pt):
+            out_ref[j * size:(j + 1) * size, :] = result[j].T.astype(jnp.bfloat16)
+    with SCOPE("drain"):
+        for copy, cond in drains:
+            when(cond, copy.wait_send)
 
 
 def per_device(start_vectors, tiles, tile_rows, tile_cols, tile_counts, center, half_width):
@@ -466,9 +470,8 @@
         + [
             pltpu.VMEM((piece_rows, vec), bf), pltpu.VMEM((pt, vec, size), f32),
             pltpu.VMEM((slots, size, size), bf),
-            pltpu.VMEM((2, 1, slots), i32), pltpu.VMEM((4, size), i32),
-            pltpu.SMEM((1, slots), i32), pltpu.SMEM((1, slots), i32), pltpu.SMEM((4, size), i32),
-            pltpu.SemaphoreType.DMA((7,)),
+            pltpu.VMEM((4, size), i32), pltpu.SMEM((4, size), i32),
+            pltpu.SemaphoreType.DMA((3,)),
         ]
         + [pltpu.SemaphoreType.DMA((2, CHUNKS, half + 2 * hq + 1))] * 2
         + [pltpu.SemaphoreType.DMA((2, CHUNKS, 3 * ways))]
@@ -477,7 +480,7 @@
     return pl.pallas_call(
         functools.partial(filter_kernel, (R, C, half, pt, slots, vec, size)),
         out_shape=jax.ShapeDtypeStruct((piece_rows, vec), bf),
-        in_specs=[anywhere] * 4 + [smem] * 3,
+        in_specs=[anywhere] * 2 + [smem] * 5,
         out_specs=vmem,
         scratch_shapes=scratch,
         compiler_params=pltpu.CompilerParams(
@@ -486,7 +489,7 @@
     )(start_vectors, tiles, tile_rows, tile_cols, tile_counts, center, half_width)
 
 
-VMEM_LIMIT = 66_800_000
+VMEM_LIMIT = 56_350_000
 
 
 def solution(mesh):

time: 57.7 us -> 47.9 us (0.83)
  Pallas kernels: 54 us -> 45 us
  local copies, waits for them, and re-layouts: 1.57 us -> 0.67 us
    pallas_call x1, Pallas kernels: 54 us -> 45 us  [per_device(): pl.pallas_call(functools.partial(filter_kernel, (R, C, half, pt, slots, v...]
    unnamed x1 -> x5, local copies, waits for them, and re-layouts: 1.57 us -> 0.67 us
where the time goes in v2:
time: 47.9 us; the launch traced here: 47.7 us
  Pallas kernels  45 us (94%)
  between operations  2 us (4%)
  local copies, waits for them, and re-layouts  0.67 us (1%)
    pallas_call x1, Pallas kernels, per_device(): pl.pallas_call(functools.partial(filter_kernel, (R, C, half, pt, slots, v...  45 us

profile of v2, /device:TPU:0, one launch (start us, length us, event | category | flops | bytes accessed | tf_op | source)
XLA Modules:
  0.0 47.7 jit_solution(4670456148752413397)
XLA Ops:
  1.3 0.0 copy-start
  1.3 0.0 copy-start.1
  2.0 0.0 copy-done
  2.0 0.0 copy-done.1
  2.0 45.0 %filter_steps.1 = bf16[512,128]{1,0:T(8,128)(2,1)S(1)} custom-call(bf16[512,128]{1,0:T(8,128)(2,1)} %x_ref.1, bf16[1,32,128,128]{3,2,1,0:T(8,128)(2,1)} %tiles_ref.1, s32[1,32]{1,0:T(1,128)S(1)} %copy-done, s32[1,32]{1,0:T(1,128)S(1)} %copy-done.1, s32[1,1]{1,0:T(1,128)S(6)} %copy.9.counts_ref, f32[1]{0:T(128)S(6)} %copy.10.center_ref, f32[1]{0:T(128)S(6)} %copy.11.width_ref), custom_call_target="tpu_custom_call" | custom-call | tf_op jit(solution)/shard_map/filter_steps/pallas_call | solution.py:480
  47.0 0.7 %copy.12 = bf16[512,128]{1,0:T(8,128)(2,1)} copy(bf16[512,128]{1,0:T(8,128)(2,1)S(1)} %filter_steps.1) | data formatting | bytes 262144
Async XLA Ops:
  1.3 0.7 %copy-start = (s32[1,32]{1,0:T(1,128)S(1)}, s32[1,32]{1,0:T(1,128)}, u32[]{:S(2)}) copy-start(s32[1,32]{1,0:T(1,128)} %row_of.1) | copy-start | bytes 388
  1.3 0.7 %copy-start.1 = (s32[1,32]{1,0:T(1,128)S(1)}, s32[1,32]{1,0:T(1,128)}, u32[]{:S(2)}) copy-start(s32[1,32]{1,0:T(1,128)} %col_of.1) | copy-start | bytes 388

commit v3 on v2

v3 whole, which is shorter than its diff:
```python
import contextlib
import functools

import jax
import jax.numpy as jnp
from jax import lax
from jax.experimental import pallas as pl
from jax.experimental.pallas import tpu as pltpu
from jax.sharding import PartitionSpec as P

CHUNKS = 2
UNROLL = 16
MESH_ID = pl.DeviceIdType.MESH
GATHER_TREES = (("tail3", "tail3"), ("tail3", "tail"))
REDUCE_TREES = (("tail", "tail"), ("tail", "tail"))
ORDER = (
    "GX00", "GZ00", "GF200", "XF100", "GF100", "GF101", "GX01", "GZ01", "XF200", "D00",
    "XF101", "B00", "GF201", "RX00", "XF201", "D01", "RM100", "B01", "RX01", "RM200",
    "RM201", "RM101", "E00", "GX10", "GZ10", "E01", "XF110", "GX11", "GZ11", "XF210",
    "GF210", "D10", "GF110", "GF211", "XF111", "B10", "XF211", "GF111", "RM210", "D11",
    "RX10", "B11", "RM110", "RM211", "RX11", "RM111", "E10", "E11",
)
SCOPE = contextlib.nullcontext


def parent(kind, length, dist):
    if kind == "chain":
        return dist - 1
    if kind == "tail":
        return dist - 1 if dist == length and length >= 2 else 0
    if kind == "tail3":
        return dist - 1 if dist == length and length >= 3 else 0
    return 0


def side(c, sgn, C):
    return c if sgn > 0 else C - 1 - c


def forwards_at(C, t, h, n, sgn, d):
    root = n - sgn * d
    return (
        0 <= n < C and 0 <= root < C and 0 <= n + sgn < C
        and parent(GATHER_TREES[t][h], side(C - 1 - root, sgn, C), d + 1) == d)


def way_at(C, t, h, n, sgn, d):
    dest = n + sgn * d
    if not (0 <= n < C and 0 <= dest < C):
        return None
    kind, length = REDUCE_TREES[t][h], side(dest, sgn, C)
    return parent(kind, length, d), d < length and parent(kind, length, d + 1) == d


def passes_at(C, t, h, n, sgn, d):
    on = way_at(C, t, h, n, sgn, d)
    return on is not None and on[1]


def arrivals(C, K, hq):
    through, count = {}, 0
    for t in range(2):
        for h in range(K):
            at = hq + 4
            for kind, test in (("gather", forwards_at), ("reduce", passes_at)):
                for d in range(1, C - 1):
                    users = [{n for n in range(C) if test(C, t, h, n, sgn, d)} for sgn in (1, -1)]
                    through[t, h, kind, 1, d] = at
                    at += bool(users[0]) and bool(users[0] & users[1])
                    through[t, h, kind, -1, d] = at
                    at += bool(users[0] | users[1])
            count = max(count, at)
    return through, count


def default_order(K, C):
    order = []
    for h in range(K):
        order += [("GX", 0, h), ("GZ", 0, h)]
    for t in range(2):
        for h in range(K):
            order += [("XF1", t, h), ("XF2", t, h), ("GF1", t, h), ("D", t, h)]
        for h in range(K):
            order += [("GF2", t, h), ("RM2", t, h), ("RM1", t, h), ("B", t, h), ("RX", t, h)]
        for h in range(K):
            order.append(("E", t, h))
            if t == 0:
                order += [("GX", 1, h), ("GZ", 1, h)]
    return order


def full_order(K, C, hq):
    base = [(s[:-2], int(s[-2]), int(s[-1])) for s in ORDER] or default_order(K, C)
    known = set(base)
    order = []
    for name, t, h in base:
        extra = []
        if name == "D":
            extra = ["XF%d" % d for d in range(1, hq + 1)]
        elif name == "B":
            extra = ["GF%d" % d for d in range(1, C - 1)]
        elif name == "E":
            extra = ["RM%d" % d for d in range(C - 2, 0, -1)]
        order += [(e, t, h) for e in extra if (e, t, h) not in known]
        if name[:2] in ("XF", "GF", "RM") and int(name[2:]) > (hq if name[:2] == "XF" else C - 2):
            continue
        order.append((name, t, h))
    return order


def filter_kernel(
    dims, x_ref, tiles_ref, rows_ref, cols_ref, counts_ref, center_ref, width_ref, out_ref, *scratch,
):
    R, C, half, pt, slots, vec, size = dims
    K = CHUNKS
    vc = vec // K
    hq = half // 2
    ways = 2 * (C - 1)
    it = iter(scratch)

    def pair():
        return [[next(it) for _ in range(K)] for _ in range(2)]

    win, seg, pair_out, row_out, pair_in, row_in = pair(), pair(), pair(), pair(), pair(), pair()
    col_out, col_fin, col_mid = pair(), pair(), pair()
    back = [next(it) for _ in range(K)]
    direct = [next(it) for _ in range(K)]
    x_in, result, tiles, flipped, spare = next(it), next(it), next(it), next(it), next(it)
    table, row_of, col_of, links = next(it), next(it), next(it), next(it)
    local, sent, arrived = next(it), next(it), next(it)

    r = lax.axis_index("row")
    c = lax.axis_index("col")
    k = lax.rem(r, 2)
    partner = r + 1 - 2 * k

    def among(test):
        members = [n for n in range(C) if test(n)]
        if len(members) in (0, C):
            return members, bool(members)
        cond = None
        for lo in members:
            if lo - 1 in members:
                continue
            hi = lo
            while hi + 1 in members:
                hi += 1
            one = c == lo if lo == hi else c <= hi if lo == 0 else c >= lo if hi == C - 1 else (c >= lo) & (c <= hi)
            cond = one if cond is None else cond | one
        return members, cond

    everyone = (list(range(C)), True)

    def when(cond, act):
        if cond is True:
            act()
        elif cond is not False:
            pl.when(cond)(act)

    def pick(test, yes, no):
        cond = among(test)[1]
        return yes if cond is True else no if cond is False else jnp.where(cond, yes, no)

    forwards = functools.partial(forwards_at, C)
    way_on = functools.partial(way_at, C)
    EVEN, ODD, PAIR, LAST, PIECES = 0, hq, hq + 1, hq + 2, hq + 3
    through, _ = arrivals(C, K, hq)

    barrier = pltpu.get_barrier_semaphore()
    row_peers = sorted({d % R for d in range(2, half + 1, 2)} | {-d % R for d in range(2, half + 1, 2)})
    for off in row_peers:
        pl.semaphore_signal(barrier, inc=1, device_id={"row": lax.rem(r + off, R)}, device_id_type=MESH_ID)
    pl.semaphore_signal(barrier, inc=1, device_id={"row": partner}, device_id_type=MESH_ID)
    for off in range(1, C):
        pl.semaphore_signal(barrier, inc=1, device_id={"col": lax.rem(c + off, C)}, device_id_type=MESH_ID)

    load_x = pltpu.make_async_copy(x_ref, x_in, local.at[0])
    load_x.start()
    load_rows = pltpu.make_async_copy(rows_ref, row_of, local.at[3])
    load_rows.start()
    load_cols = pltpu.make_async_copy(cols_ref, col_of, local.at[4])
    load_cols.start()
    fetch = pltpu.make_async_copy(tiles_ref.at[0], tiles, local.at[1])
    fetch.start()

    def way(sgn, d):
        return 2 * (d - 1) + (0 if sgn > 0 else 1)

    def tiles_at(ref, slot):
        return ref.at[pl.ds(slot * pt, pt)]

    sgns = (1, -1)
    dists = range(1, C)
    final = {}
    for t in range(2):
        for h in range(K):
            for sgn in sgns:
                for d in dists:
                    members, cond = among(lambda n: way_on(t, h, n - sgn * d, sgn, d) is not None
                                          and way_on(t, h, n - sgn * d, sgn, d)[0] == 0)
                    final[t, h, sgn, d] = members, cond
                    if cond is not True and cond is not False:
                        def clear(t=t, h=h, sgn=sgn, d=d):
                            tiles_at(col_fin[t][h], way(sgn, d))[...] = jnp.zeros((pt, vc, size), jnp.bfloat16)
                        pl.when(jnp.logical_not(cond))(clear)
            tiles_at(pair_in[t][h], hq)[...] = jnp.zeros((pt, vc, size), jnp.bfloat16)
    for h in range(K):
        back[h][slots] = jnp.zeros((vc, size), jnp.float32)
        direct[h][slots] = jnp.zeros((vc, size), jnp.float32)

    with SCOPE("loadx"):
        load_x.wait()
    for j in range(pt):
        block = x_in[j * size:(j + 1) * size, :].astype(jnp.float32).T.astype(jnp.bfloat16)
        for h in range(K):
            part = block[h * vc:(h + 1) * vc, :]
            win[0][h][j] = part
            seg[0][h][c * pt + j] = part
    with SCOPE("greet"):
        pl.semaphore_wait(barrier, len(row_peers) + 1 + C - 1)

    sends = [0] * C

    def start(copy, whom=everyone):
        when(whom[1], copy.start)
        for n in whom[0]:
            sends[n] += 1

    def to_row(src, dst, t, h, sem, row):
        return pltpu.make_async_remote_copy(
            src_ref=src, dst_ref=dst, send_sem=sent, recv_sem=arrived.at[t, h, sem],
            device_id={"row": row}, device_id_type=MESH_ID)

    def to_col(src, dst, t, h, sem, col):
        return pltpu.make_async_remote_copy(
            src_ref=src, dst_ref=dst, send_sem=sent, recv_sem=arrived.at[t, h, sem],
            device_id={"col": col}, device_id_type=MESH_ID)

    def pieces(count):
        view = tiles_at(spare, 0) if count == 1 else spare.at[pl.ds(0, count * pt)]
        return view

    def await_pieces(t, h, sem, count):
        to_row(pieces(count), pieces(count), t, h, sem, partner).wait_recv()

    def by_count(counts, act):
        for count in sorted(set(counts) - {0}):
            when(among(lambda n: counts[n] == count)[1], lambda: act(count))

    def up(d):
        return lax.rem(r + d, R)

    def start_row(t, h):
        own = tiles_at(win[t][h], 0)
        for d in range(hq, 0, -1):
            start(to_row(own, tiles_at(win[t][h], 2 * d), t, h, EVEN + d - 1, up(R - 2 * d)))
        pl.when(k == 1)(to_row(own, tiles_at(win[t][h], 1), t, h, ODD, partner).start)

    def forward_row(t, h, d):
        await_pieces(t, h, EVEN + d - 1, 1)
        view = tiles_at(win[t][h], 2 * d)
        copy = to_row(view, tiles_at(win[t][h], 2 * d - 1 + 2 * k), t, h, ODD, partner)
        if d < hq:
            start(copy)
        else:
            pl.when(k == 0)(copy.start)
            for n in range(C):
                sends[n] += 1

    def col_piece(t, h, sgn, d, hop):
        view = tiles_at(seg[t][h], c - sgn * d)
        src = view if d else tiles_at(win[t][h], 0)
        sem = pick(lambda n: forwards(t, h, n + sgn * hop, sgn, d + hop),
                   through.get((t, h, "gather", sgn, d + hop), 0), PIECES)
        return to_col(src, view, t, h, sem, c + sgn * hop)

    def start_col(t, h):
        for hop in reversed(dists):
            for sgn in sgns:
                def test(n):
                    return 0 <= n + sgn * hop < C and parent(GATHER_TREES[t][h], side(C - 1 - n, sgn, C), hop) == 0
                whom = among(test)
                if whom[0]:
                    start(col_piece(t, h, sgn, 0, hop), whom)

    def forward_col(t, h, d):
        for sgn in sgns:
            whom = among(lambda n: forwards(t, h, n, sgn, d))
            if whom[0]:
                when(whom[1], lambda: await_pieces(t, h, through[t, h, "gather", sgn, d], 1))
                start(col_piece(t, h, sgn, d, 1), whom)

    def products(source, index_ref, link_row, sums, weights):
        def one(s, carry):
            term = lax.dot_general(
                source[index_ref[0, s]], weights[s], (((1,), (0,)), ((), ())),
                preferred_element_type=jnp.float32)
            sums[s] = sums[links[link_row, s]] + term
            return carry

        lax.fori_loop(0, slots, one, 0, unroll=UNROLL)

    def pass_on(t, h, d, want):
        for sgn in sgns:
            found = sorted({way_on(t, h, n, sgn, d) for n in range(C)} - {None})
            for left, helped in found:
                if helped != want:
                    continue
                whom = among(lambda n: way_on(t, h, n, sgn, d) == (left, helped))
                w = way(sgn, d)

                def act():
                    if helped:
                        await_pieces(t, h, through[t, h, "reduce", sgn, d], 1)
                    dest = c + sgn * d
                    for j in range(pt):
                        value = direct[h][links[2, dest * pt + j]]
                        if helped:
                            value += col_mid[t][h][w * pt + j].astype(jnp.float32)
                        col_out[t][h][w * pt + j] = value.astype(jnp.bfloat16)
                when(whom[1], act)
                src = tiles_at(col_out[t][h], w)
                if left == 0:
                    copy = to_col(src, tiles_at(col_fin[t][h], w), t, h, LAST, c + sgn * d)
                else:
                    copy = to_col(src, tiles_at(col_mid[t][h], way(sgn, left)), t, h,
                                  through[t, h, "reduce", sgn, left], c + sgn * (d - left))
                start(copy, whom)

    def do_direct(t, h):
        await_pieces(t, h, ODD, hq)
        products(win[t][h], col_of, 0, direct[h], flipped)
        for d in reversed(dists):
            pass_on(t, h, d, False)

    def do_back(t, h):
        held = [sum(forwards(t, h, n, sgn, d) for sgn in sgns for d in dists) for n in range(C)]
        by_count([C - 1 - held[n] for n in range(C)], lambda count: await_pieces(t, h, PIECES, count))
        products(seg[t][h], row_of, 1, back[h], tiles)
        for i in range(1, hq + 1):
            for j in range(pt):
                pair_out[t][h][(i - 1) * pt + j] = back[h][links[3, (2 * i - 1) * pt + j]].astype(jnp.bfloat16)
            start(to_row(tiles_at(pair_out[t][h], i - 1), tiles_at(pair_in[t][h], i - 1), t, h, PAIR, partner))

    def return_row(t, h):
        await_pieces(t, h, PAIR, hq)
        for d in range(hq, 0, -1):
            for j in range(pt):
                value = back[h][links[3, 2 * d * pt + j]] + pair_in[t][h][(d - 1 + k) * pt + j].astype(jnp.float32)
                row_out[t][h][(d - 1) * pt + j] = value.astype(jnp.bfloat16)
            start(to_row(tiles_at(row_out[t][h], d - 1), tiles_at(row_in[t][h], d - 1), t, h, LAST, up(2 * d)))

    shift = center_ref[0]
    width = width_ref[0]

    def finish(t, h):
        ends = [hq + sum(n in final[t, h, sgn, d][0] for sgn in sgns for d in dists) for n in range(C)]
        by_count(ends, lambda count: await_pieces(t, h, LAST, count))
        slot = jnp.where(k == 1, 0, hq)
        for j in range(pt):
            total = back[h][links[3, j]] + direct[h][links[2, c * pt + j]]
            total += pair_in[t][h][slot * pt + j].astype(jnp.float32)
            for d in range(hq):
                total += row_in[t][h][d * pt + j].astype(jnp.float32)
            for sgn in sgns:
                for d in dists:
                    if final[t, h, sgn, d][0]:
                        total += col_fin[t][h][way(sgn, d) * pt + j].astype(jnp.float32)
            begin = win[0][h][j].astype(jnp.float32)
            if t == 0:
                first = ((total - shift * begin) / width).astype(jnp.bfloat16)
                win[1][h][j] = first
                seg[1][h][c * pt + j] = first
            else:
                first = win[1][h][j].astype(jnp.float32)
                result[j, h * vc:(h + 1) * vc, :] = 2.0 * (total - shift * first) / width - begin

    def link_slots():
        load_rows.wait()
        load_cols.wait()
        count = counts_ref[0, 0]
        sub = lax.broadcasted_iota(jnp.int32, (slots, size), 0)
        lane = lax.broadcasted_iota(jnp.int32, (slots, size), 1)
        for i, keys in enumerate((row_of, col_of)):
            key = jnp.full((slots, size), -1, jnp.int32)
            column = key
            for s in range(slots):
                one = keys[0, s]
                key = jnp.where(lane == s, one, key)
                column = jnp.where(sub == s, one, column)
            used = sub < count
            same = (column == key) & (sub < lane) & used
            before = jnp.max(jnp.where(same, sub, -1), axis=0, keepdims=True)
            table[i:i + 1, :] = jnp.where(before < 0, slots, before)
            last = jnp.max(jnp.where((column == lane) & used, sub, -1), axis=0, keepdims=True)
            table[2 + i:3 + i, :] = jnp.where(last < 0, slots, last)
        publish = pltpu.make_async_copy(table, links, local.at[2])
        publish.start()
        fetch.wait()

        def flip(s, carry):
            flipped[s] = tiles[s].astype(jnp.float32).T.astype(jnp.bfloat16)
            return carry

        lax.fori_loop(0, slots, flip, 0, unroll=UNROLL)
        publish.wait()

    acts = {"GX": start_row, "GZ": start_col, "D": do_direct, "B": do_back, "RX": return_row, "E": finish}
    linked = 0
    for name, t, h in full_order(K, C, hq):
        with SCOPE("%s_%d%d" % (name, t, h)):
            if name in acts:
                acts[name](t, h)
            elif name[:2] == "RM":
                pass_on(t, h, int(name[2:]), True)
            else:
                (forward_row if name[:2] == "XF" else forward_col)(t, h, int(name[2:]))
        linked += (name, t, h) in (("GX", 0, 0), ("GZ", 0, 0))
        if linked == 2:
            with SCOPE("link"):
                link_slots()
            linked += 1
    with SCOPE("out"):
        for j in range(pt):
            out_ref[j * size:(j + 1) * size, :] = result[j].T.astype(jnp.bfloat16)
    with SCOPE("drain"):
        by_count(sends, lambda count: to_row(pieces(count), pieces(count), 0, 0, 0, partner).wait_send())


def per_device(start_vectors, tiles, tile_rows, tile_cols, tile_counts, center, half_width):
    R = lax.axis_size("row")
    C = lax.axis_size("col")
    half = R // 2
    hq = half // 2
    piece_rows, vec = start_vectors.shape
    size = tiles.shape[-1]
    slots = tiles.shape[1]
    pt = piece_rows // size
    vc = vec // CHUNKS
    ways = 2 * (C - 1)
    nsem = arrivals(C, CHUNKS, hq)[1]
    most = 2 * CHUNKS * (4 * hq + 4 * C)
    smem = pl.BlockSpec(memory_space=pltpu.SMEM)
    vmem = pl.BlockSpec(memory_space=pltpu.VMEM)
    anywhere = pl.BlockSpec(memory_space=pl.ANY)
    bf, f32, i32 = jnp.bfloat16, jnp.float32, jnp.int32

    def pair(count):
        return [pltpu.VMEM((count * pt, vc, size), bf) for _ in range(2 * CHUNKS)]

    scratch = (
        pair(half + 1) + pair(C) + pair(hq) + pair(hq) + pair(hq + 1) + pair(hq)
        + pair(ways) + pair(ways) + pair(ways)
        + [pltpu.VMEM((slots + 1, vc, size), f32) for _ in range(2 * CHUNKS)]
        + [
            pltpu.VMEM((piece_rows, vec), bf), pltpu.VMEM((pt, vec, size), f32),
            pltpu.VMEM((slots, size, size), bf), pltpu.VMEM((slots, size, size), bf),
            pltpu.VMEM((most * pt, vc, size), bf),
            pltpu.VMEM((4, size), i32),
            pltpu.SMEM((1, slots), i32), pltpu.SMEM((1, slots), i32), pltpu.SMEM((4, size), i32),
        ]
        + [pltpu.SemaphoreType.DMA((5,)), pltpu.SemaphoreType.DMA, pltpu.SemaphoreType.DMA((2, CHUNKS, nsem))]
    )
    return pl.pallas_call(
        functools.partial(filter_kernel, (R, C, half, pt, slots, vec, size)),
        out_shape=jax.ShapeDtypeStruct((piece_rows, vec), bf),
        in_specs=[anywhere] * 4 + [smem] * 3,
        out_specs=vmem,
        scratch_shapes=scratch,
        compiler_params=pltpu.CompilerParams(
            collective_id=0, has_side_effects=True, vmem_limit_bytes=VMEM_LIMIT),
        name="filter_steps",
    )(start_vectors, tiles, tile_rows, tile_cols, tile_counts, center, half_width)


VMEM_LIMIT = 56_350_000


def solution(mesh):
    return jax.shard_map(
        per_device,
        mesh=mesh,
        in_specs=(
            P(("row", "col"), None),
            P("row", "col", None, None),
            P("row", "col"),
            P("row", "col"),
            P("row", "col"),
            P(),
            P(),
        ),
        out_specs=P(("row", "col"), None),
        check_vma=False,
    )
```

time: 47.9 us -> 46 us (0.960)
  Pallas kernels: 45 us -> 43.2 us
    pallas_call x1, Pallas kernels: 45 us -> 43.2 us  [per_device(): pl.pallas_call(functools.partial(filter_kernel, (R, C, half, pt, slots, v...]
where the time goes in v3:
time: 46 us; the launch traced here: 45.8 us
  Pallas kernels  43.2 us (94%)
  between operations  2 us (4%)
  local copies, waits for them, and re-layouts  0.67 us (1%)
    pallas_call x1, Pallas kernels, per_device(): pl.pallas_call(functools.partial(filter_kernel, (R, C, half, pt, slots, v...  43.2 us

profile of v3, /device:TPU:0, one launch (start us, length us, event | category | flops | bytes accessed | tf_op | source)
XLA Modules:
  0.0 45.8 jit_solution(2013948400176324375)
XLA Ops:
  1.3 0.0 copy-start
  1.3 0.0 copy-start.1
  2.0 0.0 copy-done
  2.0 0.0 copy-done.1
  2.0 43.2 %filter_steps.1 = bf16[512,128]{1,0:T(8,128)(2,1)S(1)} custom-call(bf16[512,128]{1,0:T(8,128)(2,1)} %x_ref.1, bf16[1,32,128,128]{3,2,1,0:T(8,128)(2,1)} %tiles_ref.1, s32[1,32]{1,0:T(1,128)S(1)} %copy-done, s32[1,32]{1,0:T(1,128)S(1)} %copy-done.1, s32[1,1]{1,0:T(1,128)S(6)} %copy.9.counts_ref, f32[1]{0:T(128)S(6)} %copy.10.center_ref, f32[1]{0:T(128)S(6)} %copy.11.width_ref), custom_call_target="tpu_custom_call" | custom-call | tf_op jit(solution)/shard_map/filter_steps/pallas_call | solution.py:464
  45.2 0.7 %copy.12 = bf16[512,128]{1,0:T(8,128)(2,1)} copy(bf16[512,128]{1,0:T(8,128)(2,1)S(1)} %filter_steps.1) | data formatting | bytes 262144
Async XLA Ops:
  1.3 0.7 %copy-start = (s32[1,32]{1,0:T(1,128)S(1)}, s32[1,32]{1,0:T(1,128)}, u32[]{:S(2)}) copy-start(s32[1,32]{1,0:T(1,128)} %rows_ref.1) | copy-start | bytes 388
  1.3 0.7 %copy-start.1 = (s32[1,32]{1,0:T(1,128)S(1)}, s32[1,32]{1,0:T(1,128)}, u32[]{:S(2)}) copy-start(s32[1,32]{1,0:T(1,128)} %cols_ref.1) | copy-start | bytes 388

commit v4 on v3

--- a/solution.py
+++ b/solution.py
@@ -11,14 +11,14 @@
 CHUNKS = 2
 UNROLL = 16
 MESH_ID = pl.DeviceIdType.MESH
-GATHER_TREES = (("tail3", "tail3"), ("tail3", "tail"))
-REDUCE_TREES = (("tail", "tail"), ("tail", "tail"))
+GATHER_TREES = (("tail3", "tail3"), ("tail3", "tail3"))
+REDUCE_TREES = (("tail3", "tail"), ("tail", "tail"))
 ORDER = (
-    "GX00", "GZ00", "GF200", "XF100", "GF100", "GF101", "GX01", "GZ01", "XF200", "D00",
-    "XF101", "B00", "GF201", "RX00", "XF201", "D01", "RM100", "B01", "RX01", "RM200",
-    "RM201", "RM101", "E00", "GX10", "GZ10", "E01", "XF110", "GX11", "GZ11", "XF210",
-    "GF210", "D10", "GF110", "GF211", "XF111", "B10", "XF211", "GF111", "RM210", "D11",
-    "RX10", "B11", "RM110", "RM211", "RX11", "RM111", "E10", "E11",
+    "GZ00", "GX00", "GF100", "GF101", "GZ01", "GF200", "GF201", "XF100", "GX01", "XF200",
+    "D00", "B00", "XF201", "XF101", "RM200", "RX00", "RM100", "D01", "B01", "RM201",
+    "RM101", "RX01", "E00", "GZ10", "GX10", "GF210", "E01", "GZ11", "GX11", "XF210",
+    "XF110", "GF211", "D10", "GF110", "XF111", "B10", "XF211", "D11", "RM210", "RX10",
+    "GF111", "B11", "RM110", "RM211", "RX11", "RM111", "E10", "E11",
 )
 SCOPE = contextlib.nullcontext
 

time: 46 us -> 42.3 us (0.920)
  Pallas kernels: 43.2 us -> 39.5 us
    pallas_call x1, Pallas kernels: 43.2 us -> 39.5 us  [per_device(): pl.pallas_call(functools.partial(filter_kernel, (R, C, half, pt, slots, v...]
where the time goes in v4:
time: 42.3 us; the launch traced here: 42.2 us
  Pallas kernels  39.5 us (93%)
  between operations  2 us (5%)
  local copies, waits for them, and re-layouts  0.67 us (2%)
    pallas_call x1, Pallas kernels, per_device(): pl.pallas_call(functools.partial(filter_kernel, (R, C, half, pt, slots, v...  39.5 us

profile of v4, /device:TPU:0, one launch (start us, length us, event | category | flops | bytes accessed | tf_op | source)
XLA Modules:
  0.0 42.2 jit_solution(12635227664380687479)
XLA Ops:
  1.3 0.0 copy-start
  1.3 0.0 copy-start.1
  2.0 0.0 copy-done
  2.0 0.0 copy-done.1
  2.0 39.5 %filter_steps.1 = bf16[512,128]{1,0:T(8,128)(2,1)S(1)} custom-call(bf16[512,128]{1,0:T(8,128)(2,1)} %x_ref.1, bf16[1,32,128,128]{3,2,1,0:T(8,128)(2,1)} %tiles_ref.1, s32[1,32]{1,0:T(1,128)S(1)} %copy-done, s32[1,32]{1,0:T(1,128)S(1)} %copy-done.1, s32[1,1]{1,0:T(1,128)S(6)} %copy.9.counts_ref, f32[1]{0:T(128)S(6)} %copy.10.center_ref, f32[1]{0:T(128)S(6)} %copy.11.width_ref), custom_call_target="tpu_custom_call" | custom-call | tf_op jit(solution)/shard_map/filter_steps/pallas_call | solution.py:464
  41.5 0.7 %copy.12 = bf16[512,128]{1,0:T(8,128)(2,1)} copy(bf16[512,128]{1,0:T(8,128)(2,1)S(1)} %filter_steps.1) | data formatting | bytes 262144
Async XLA Ops:
  1.3 0.7 %copy-start = (s32[1,32]{1,0:T(1,128)S(1)}, s32[1,32]{1,0:T(1,128)}, u32[]{:S(2)}) copy-start(s32[1,32]{1,0:T(1,128)} %rows_ref.1) | copy-start | bytes 388
  1.3 0.7 %copy-start.1 = (s32[1,32]{1,0:T(1,128)S(1)}, s32[1,32]{1,0:T(1,128)}, u32[]{:S(2)}) copy-start(s32[1,32]{1,0:T(1,128)} %cols_ref.1) | copy-start | bytes 388

commit v5 on v4

v5 whole, which is shorter than its diff:
```python
import contextlib
import functools

import jax
import jax.numpy as jnp
from jax import lax
from jax.experimental import pallas as pl
from jax.experimental.pallas import tpu as pltpu
from jax.sharding import PartitionSpec as P

SHARES = (1, 1)
CHUNKS = len(SHARES)
GRAIN = 16
PARTS = 1
UNROLL = 16
MESH_ID = pl.DeviceIdType.MESH
GATHER_TREES = ((("tail3",), ("tail3",)), (("tail3",), ("tail3",)))
REDUCE_TREES = ((("tail",), ("tail",)), (("tail",), ("tail",)))
ORDER = (
    "GZ000", "GX00", "GZ001", "XF100", "GX01", "GF2S000", "XF200", "D00", "XF101", "XF201",
    "GF2S001", "D01", "RM1L000", "RM2L000", "B00", "RX00", "RM2L001", "B01", "RM1L001", "RX01",
    "E00", "GZ010", "GX10", "GF2S010", "E01", "GZ011", "GX11", "XF110", "XF210", "GF2S011",
    "D10", "XF111", "XF211", "B10", "D11", "RM1L010", "RX10", "RM2L010", "B11", "RM2L011",
    "RX11", "RM1L011", "E10", "E11",
)
SCOPE = contextlib.nullcontext


def widths(vec):
    return [vec * share // sum(SHARES) for share in SHARES]


def parts_of(pt):
    return PARTS if pt % PARTS == 0 else 1


def parent(kind, length, dist):
    if kind == "chain":
        return dist - 1
    if kind == "tail":
        return dist - 1 if dist == length and length >= 2 else 0
    if kind == "tail3":
        return dist - 1 if dist == length and length >= 3 else 0
    return 0


def side(c, sgn, C):
    return c if sgn > 0 else C - 1 - c


def is_long(C, n, sgn):
    return (2 * n < C) == (sgn > 0)


def forwards_at(C, t, h, u, n, sgn, d):
    root = n - sgn * d
    return (
        0 <= n < C and 0 <= root < C and 0 <= n + sgn < C
        and parent(GATHER_TREES[t][h][u], side(C - 1 - root, sgn, C), d + 1) == d)


def way_at(C, t, h, u, n, sgn, d):
    dest = n + sgn * d
    if not (0 <= n < C and 0 <= dest < C):
        return None
    kind, length = REDUCE_TREES[t][h][u], side(dest, sgn, C)
    return parent(kind, length, d), d < length and parent(kind, length, d + 1) == d


def passes_at(C, t, h, u, n, sgn, d):
    on = way_at(C, t, h, u, n, sgn, d)
    return on is not None and on[1]


def arrivals(C, K, hq, parts):
    through, count = {}, 0
    for t in range(2):
        for h in range(K):
            at = hq + 4
            for u in range(parts):
                for kind, test in (("gather", forwards_at), ("reduce", passes_at)):
                    for d in range(1, C - 1):
                        users = [{n for n in range(C) if test(C, t, h, u, n, sgn, d)} for sgn in (1, -1)]
                        through[t, h, u, kind, 1, d] = at
                        at += bool(users[0]) and bool(users[0] & users[1])
                        through[t, h, u, kind, -1, d] = at
                        at += bool(users[0] | users[1])
            count = max(count, at)
    return through, count


def parse(word):
    name, t, h = word[:-2], int(word[-2]), int(word[-1])
    kind = name[:2]
    if kind in ("XF", "GZ"):
        return kind, t, h, int(name[2:])
    if kind in ("GF", "RM"):
        return kind, t, h, int(name[2]), name[3], int(name[4])
    return name, t, h


def default_order(K, parts):
    order = []
    for h in range(K):
        order += [("GX", 0, h)] + [("GZ", 0, h, u) for u in range(parts)]
    for t in range(2):
        order += [("D", t, h) for h in range(K)]
        for h in range(K):
            order += [("B", t, h), ("RX", t, h)]
        for h in range(K):
            order.append(("E", t, h))
            if t == 0:
                order += [("GX", 1, h)] + [("GZ", 1, h, u) for u in range(parts)]
    return order


def full_order(K, C, hq, parts):
    base = [parse(word) for word in ORDER] or default_order(K, parts)
    known = set(base)
    order = []
    for task in base:
        kind, t, h = task[:3]
        extra = []
        if kind == "D":
            extra = [("XF", t, h, d) for d in range(1, hq + 1)]
        elif kind == "B":
            extra = [("GF", t, h, d, rel, u) for d in range(1, C - 1) for u in range(parts) for rel in "LS"]
        elif kind == "E":
            extra = [("RM", t, h, d, rel, u) for d in range(C - 2, 0, -1) for u in range(parts) for rel in "LS"]
        order += [e for e in extra if e not in known]
        if kind == "XF" and task[3] > hq or kind in ("GF", "RM") and task[3] > C - 2:
            continue
        if kind in ("GZ", "GF", "RM") and task[-1] >= parts:
            continue
        order.append(task)
    return order


def filter_kernel(
    dims, x_ref, tiles_ref, rows_ref, cols_ref, used_ref, shift_ref, scale_ref, out_ref, *scratch,
):
    R, C, half, pt, slots, vec, size = dims
    K = CHUNKS
    vcs = widths(vec)
    begins = [sum(vcs[:h]) for h in range(K)]
    hq = half // 2
    ways = 2 * (C - 1)
    parts = parts_of(pt)
    ptu = pt // parts
    it = iter(scratch)

    def pair():
        return [[next(it) for _ in range(K)] for _ in range(2)]

    win, seg, pair_out, row_out, pair_in, row_in = pair(), pair(), pair(), pair(), pair(), pair()
    col_out, col_fin, col_mid = pair(), pair(), pair()
    back = [next(it) for _ in range(K)]
    direct = [next(it) for _ in range(K)]
    x_in, result, tiles, flipped, spare = next(it), next(it), next(it), next(it), next(it)
    table, row_of, col_of = next(it), next(it), next(it)
    counts_ref, center_ref, width_ref, links = next(it), next(it), next(it), next(it)
    local, sent, arrived = next(it), next(it), next(it)

    r = lax.axis_index("row")
    c = lax.axis_index("col")
    k = lax.rem(r, 2)
    partner = r + 1 - 2 * k

    def among(test):
        members = [n for n in range(C) if test(n)]
        if len(members) in (0, C):
            return members, bool(members)
        cond = None
        for lo in members:
            if lo - 1 in members:
                continue
            hi = lo
            while hi + 1 in members:
                hi += 1
            one = c == lo if lo == hi else c <= hi if lo == 0 else c >= lo if hi == C - 1 else (c >= lo) & (c <= hi)
            cond = one if cond is None else cond | one
        return members, cond

    everyone = (list(range(C)), True)

    def when(cond, act):
        if cond is True:
            act()
        elif cond is not False:
            pl.when(cond)(act)

    def pick(test, yes, no):
        cond = among(test)[1]
        return yes if cond is True else no if cond is False else jnp.where(cond, yes, no)

    forwards = functools.partial(forwards_at, C)
    way_on = functools.partial(way_at, C)
    EVEN, ODD, PAIR, LAST, PIECES = 0, hq, hq + 1, hq + 2, hq + 3
    through, _ = arrivals(C, K, hq, parts)

    barrier = pltpu.get_barrier_semaphore()
    row_peers = sorted({d % R for d in range(2, half + 1, 2)} | {-d % R for d in range(2, half + 1, 2)})
    for off in row_peers:
        pl.semaphore_signal(barrier, inc=1, device_id={"row": lax.rem(r + off, R)}, device_id_type=MESH_ID)
    pl.semaphore_signal(barrier, inc=1, device_id={"row": partner}, device_id_type=MESH_ID)
    for off in range(1, C):
        pl.semaphore_signal(barrier, inc=1, device_id={"col": lax.rem(c + off, C)}, device_id_type=MESH_ID)

    load_x = pltpu.make_async_copy(x_ref, x_in, local.at[0])
    load_x.start()
    small = (
        (rows_ref, row_of), (cols_ref, col_of), (used_ref, counts_ref), (shift_ref, center_ref), (scale_ref, width_ref))
    loads = [pltpu.make_async_copy(src, dst, local.at[3 + i]) for i, (src, dst) in enumerate(small)]
    for copy in loads:
        copy.start()
    fetch = pltpu.make_async_copy(tiles_ref.at[0], tiles, local.at[1])
    fetch.start()

    def way(sgn, d):
        return 2 * (d - 1) + (0 if sgn > 0 else 1)

    def tiles_at(ref, slot):
        return ref.at[pl.ds(slot * pt, pt)]

    def part_at(ref, slot, u):
        return ref.at[pl.ds(slot * pt + u * ptu, ptu)]

    sgns = (1, -1)
    dists = range(1, C)
    final = {}
    for t in range(2):
        for h in range(K):
            for u in range(parts):
                for sgn in sgns:
                    for d in dists:
                        def test(n):
                            on = way_on(t, h, u, n - sgn * d, sgn, d)
                            return on is not None and on[0] == 0
                        members, cond = final[t, h, u, sgn, d] = among(test)
                        if cond is not True and cond is not False:
                            def clear():
                                part_at(col_fin[t][h], way(sgn, d), u)[...] = jnp.zeros(
                                    (ptu, vcs[h], size), jnp.bfloat16)
                            pl.when(jnp.logical_not(cond))(clear)
            tiles_at(pair_in[t][h], hq)[...] = jnp.zeros((pt, vcs[h], size), jnp.bfloat16)
    for h in range(K):
        back[h][slots] = jnp.zeros((vcs[h], size), jnp.float32)
        direct[h][slots] = jnp.zeros((vcs[h], size), jnp.float32)

    with SCOPE("loadx"):
        load_x.wait()
    for j in range(pt):
        block = x_in[j * size:(j + 1) * size, :].astype(jnp.float32).T.astype(jnp.bfloat16)
        for h in range(K):
            part = block[begins[h]:begins[h] + vcs[h], :]
            win[0][h][j] = part
            seg[0][h][c * pt + j] = part
    with SCOPE("greet"):
        pl.semaphore_wait(barrier, len(row_peers) + 1 + C - 1)

    sends = [0] * C

    def grains(count, h):
        return count * ptu * (vcs[h] // GRAIN)

    def start(copy, h, whom=everyone, count=parts):
        when(whom[1], copy.start)
        for n in whom[0]:
            sends[n] += grains(count, h)

    def to_row(src, dst, t, h, sem, row):
        return pltpu.make_async_remote_copy(
            src_ref=src, dst_ref=dst, send_sem=sent, recv_sem=arrived.at[t, h, sem],
            device_id={"row": row}, device_id_type=MESH_ID)

    def to_col(src, dst, t, h, sem, col):
        return pltpu.make_async_remote_copy(
            src_ref=src, dst_ref=dst, send_sem=sent, recv_sem=arrived.at[t, h, sem],
            device_id={"col": col}, device_id_type=MESH_ID)

    def await_pieces(t, h, sem, count):
        view = spare.at[pl.ds(0, grains(count, h))]
        to_row(view, view, t, h, sem, partner).wait_recv()

    def by_count(counts, act):
        for count in sorted(set(counts) - {0}):
            when(among(lambda n: counts[n] == count)[1], lambda: act(count))

    def up(d):
        return lax.rem(r + d, R)

    def start_row(t, h):
        own = tiles_at(win[t][h], 0)
        for d in range(hq, 0, -1):
            start(to_row(own, tiles_at(win[t][h], 2 * d), t, h, EVEN + d - 1, up(R - 2 * d)), h)
        pl.when(k == 1)(to_row(own, tiles_at(win[t][h], 1), t, h, ODD, partner).start)

    def forward_row(t, h, d):
        await_pieces(t, h, EVEN + d - 1, parts)
        view = tiles_at(win[t][h], 2 * d)
        copy = to_row(view, tiles_at(win[t][h], 2 * d - 1 + 2 * k), t, h, ODD, partner)
        if d < hq:
            start(copy, h)
        else:
            pl.when(k == 0)(copy.start)
            for n in range(C):
                sends[n] += grains(parts, h)

    def col_piece(t, h, u, sgn, d, hop):
        view = part_at(seg[t][h], c - sgn * d, u)
        src = view if d else part_at(win[t][h], 0, u)
        sem = pick(lambda n: forwards(t, h, u, n + sgn * hop, sgn, d + hop),
                   through.get((t, h, u, "gather", sgn, d + hop), 0), PIECES)
        return to_col(src, view, t, h, sem, c + sgn * hop)

    def start_col(t, h, u):
        for hop in reversed(dists):
            for sgn in sgns:
                def test(n):
                    return 0 <= n + sgn * hop < C and parent(GATHER_TREES[t][h][u], side(C - 1 - n, sgn, C), hop) == 0
                whom = among(test)
                if whom[0]:
                    start(col_piece(t, h, u, sgn, 0, hop), h, whom, 1)

    def forward_col(t, h, d, rel, u):
        for sgn in sgns:
            whom = among(lambda n: forwards(t, h, u, n, sgn, d) and is_long(C, n, sgn) == (rel == "L"))
            if whom[0]:
                when(whom[1], lambda: await_pieces(t, h, through[t, h, u, "gather", sgn, d], 1))
                start(col_piece(t, h, u, sgn, d, 1), h, whom, 1)

    def products(source, index_ref, link_row, sums, weights):
        def one(s, carry):
            term = lax.dot_general(
                source[index_ref[0, s]], weights[s], (((1,), (0,)), ((), ())),
                preferred_element_type=jnp.float32)
            sums[s] = sums[links[link_row, s]] + term
            return carry

        lax.fori_loop(0, slots, one, 0, unroll=UNROLL)

    def pass_on(t, h, d, rel, u):
        for sgn in sgns:
            found = sorted({way_on(t, h, u, n, sgn, d) for n in range(C)} - {None})
            for left, helped in found:
                if helped != bool(rel):
                    continue
                whom = among(lambda n: way_on(t, h, u, n, sgn, d) == (left, helped)
                             and (not rel or is_long(C, n, sgn) == (rel == "L")))
                if not whom[0]:
                    continue
                w = way(sgn, d)

                def act():
                    if helped:
                        await_pieces(t, h, through[t, h, u, "reduce", sgn, d], 1)
                    dest = c + sgn * d
                    for j in range(u * ptu, (u + 1) * ptu):
                        value = direct[h][links[2, dest * pt + j]]
                        if helped:
                            value += col_mid[t][h][w * pt + j].astype(jnp.float32)
                        col_out[t][h][w * pt + j] = value.astype(jnp.bfloat16)
                when(whom[1], act)
                src = part_at(col_out[t][h], w, u)
                if left == 0:
                    copy = to_col(src, part_at(col_fin[t][h], w, u), t, h, LAST, c + sgn * d)
                else:
                    copy = to_col(src, part_at(col_mid[t][h], way(sgn, left), u), t, h,
                                  through[t, h, u, "reduce", sgn, left], c + sgn * (d - left))
                start(copy, h, whom, 1)

    def do_direct(t, h):
        await_pieces(t, h, ODD, hq * parts)
        products(win[t][h], col_of, 0, direct[h], flipped)
        for u in range(parts):
            for d in reversed(dists):
                pass_on(t, h, d, "", u)

    def do_back(t, h):
        held = [sum(forwards(t, h, u, n, sgn, d) for u in range(parts) for sgn in sgns for d in dists) for n in range(C)]
        by_count([(C - 1) * parts - held[n] for n in range(C)], lambda count: await_pieces(t, h, PIECES, count))
        products(seg[t][h], row_of, 1, back[h], tiles)
        for i in range(1, hq + 1):
            for j in range(pt):
                pair_out[t][h][(i - 1) * pt + j] = back[h][links[3, (2 * i - 1) * pt + j]].astype(jnp.bfloat16)
            start(to_row(tiles_at(pair_out[t][h], i - 1), tiles_at(pair_in[t][h], i - 1), t, h, PAIR, partner), h)

    def return_row(t, h):
        await_pieces(t, h, PAIR, hq * parts)
        for d in range(hq, 0, -1):
            for j in range(pt):
                value = back[h][links[3, 2 * d * pt + j]] + pair_in[t][h][(d - 1 + k) * pt + j].astype(jnp.float32)
                row_out[t][h][(d - 1) * pt + j] = value.astype(jnp.bfloat16)
            start(to_row(tiles_at(row_out[t][h], d - 1), tiles_at(row_in[t][h], d - 1), t, h, LAST, up(2 * d)), h)


    def finish(t, h):
        ends = [hq * parts + sum(n in final[t, h, u, sgn, d][0] for u in range(parts) for sgn in sgns for d in dists)
                for n in range(C)]
        by_count(ends, lambda count: await_pieces(t, h, LAST, count))
        slot = jnp.where(k == 1, 0, hq)
        for j in range(pt):
            total = back[h][links[3, j]] + direct[h][links[2, c * pt + j]]
            total += pair_in[t][h][slot * pt + j].astype(jnp.float32)
            for d in range(hq):
                total += row_in[t][h][d * pt + j].astype(jnp.float32)
            for sgn in sgns:
                for d in dists:
                    if final[t, h, j // ptu, sgn, d][0]:
                        total += col_fin[t][h][way(sgn, d) * pt + j].astype(jnp.float32)
            begin = win[0][h][j].astype(jnp.float32)
            shift, width = center_ref[0], width_ref[0]
            if t == 0:
                first = ((total - shift * begin) / width).astype(jnp.bfloat16)
                win[1][h][j] = first
                seg[1][h][c * pt + j] = first
            else:
                first = win[1][h][j].astype(jnp.float32)
                result[j, begins[h]:begins[h] + vcs[h], :] = 2.0 * (total - shift * first) / width - begin

    def link_slots():
        for copy in loads:
            copy.wait()
        count = counts_ref[0, 0]
        sub = lax.broadcasted_iota(jnp.int32, (slots, size), 0)
        lane = lax.broadcasted_iota(jnp.int32, (slots, size), 1)
        for i, keys in enumerate((row_of, col_of)):
            key = jnp.full((slots, size), -1, jnp.int32)
            column = key
            for s in range(slots):
                one = keys[0, s]
                key = jnp.where(lane == s, one, key)
                column = jnp.where(sub == s, one, column)
            used = sub < count
            same = (column == key) & (sub < lane) & used
            before = jnp.max(jnp.where(same, sub, -1), axis=0, keepdims=True)
            table[i:i + 1, :] = jnp.where(before < 0, slots, before)
            last = jnp.max(jnp.where((column == lane) & used, sub, -1), axis=0, keepdims=True)
            table[2 + i:3 + i, :] = jnp.where(last < 0, slots, last)
        publish = pltpu.make_async_copy(table, links, local.at[2])
        publish.start()
        fetch.wait()

        def flip(s, carry):
            flipped[s] = tiles[s].astype(jnp.float32).T.astype(jnp.bfloat16)
            return carry

        lax.fori_loop(0, slots, flip, 0, unroll=UNROLL)
        publish.wait()

    acts = {
        "GX": start_row, "GZ": start_col, "XF": forward_row, "GF": forward_col, "D": do_direct, "RM": pass_on,
        "B": do_back, "RX": return_row, "E": finish}
    first = {("GX", 0, 0)} | {("GZ", 0, 0, u) for u in range(parts)}
    for kind, *args in full_order(K, C, hq, parts):
        with SCOPE(kind + "".join(str(a) for a in args)):
            acts[kind](*args)
        if first:
            first.discard((kind, *args))
            if not first:
                with SCOPE("link"):
                    link_slots()
    with SCOPE("out"):
        for j in range(pt):
            out_ref[j * size:(j + 1) * size, :] = result[j].T.astype(jnp.bfloat16)
    with SCOPE("drain"):
        def drained(count):
            view = spare.at[pl.ds(0, count)]
            to_row(view, view, 0, 0, 0, partner).wait_send()
        by_count(sends, drained)


def per_device(start_vectors, tiles, tile_rows, tile_cols, tile_counts, center, half_width):
    R = lax.axis_size("row")
    C = lax.axis_size("col")
    half = R // 2
    hq = half // 2
    piece_rows, vec = start_vectors.shape
    size = tiles.shape[-1]
    slots = tiles.shape[1]
    pt = piece_rows // size
    vcs = widths(vec)
    ways = 2 * (C - 1)
    parts = parts_of(pt)
    nsem = arrivals(C, CHUNKS, hq, parts)[1]
    most = 2 * (4 * hq + 4 * C) * pt * (vec // GRAIN)
    vmem = pl.BlockSpec(memory_space=pltpu.VMEM)
    bf, f32, i32 = jnp.bfloat16, jnp.float32, jnp.int32

    def pair(count):
        return [pltpu.VMEM((count * pt, vc, size), bf) for vc in vcs * 2]

    scratch = (
        pair(half + 1) + pair(C) + pair(hq) + pair(hq) + pair(hq + 1) + pair(hq)
        + pair(ways) + pair(ways) + pair(ways)
        + [pltpu.VMEM((slots + 1, vc, size), f32) for vc in vcs * 2]
        + [
            pltpu.VMEM((piece_rows, vec), bf), pltpu.VMEM((pt, vec, size), f32),
            pltpu.VMEM((slots, size, size), bf), pltpu.VMEM((slots, size, size), bf),
            pltpu.VMEM((most, GRAIN, size), bf),
            pltpu.VMEM((4, size), i32),
            pltpu.SMEM((1, slots), i32), pltpu.SMEM((1, slots), i32),
            pltpu.SMEM((1, 1), i32), pltpu.SMEM((1,), f32), pltpu.SMEM((1,), f32), pltpu.SMEM((4, size), i32),
        ]
        + [pltpu.SemaphoreType.DMA((8,)), pltpu.SemaphoreType.DMA, pltpu.SemaphoreType.DMA((2, CHUNKS, nsem))]
    )
    return pl.pallas_call(
        functools.partial(filter_kernel, (R, C, half, pt, slots, vec, size)),
        out_shape=jax.ShapeDtypeStruct((piece_rows, vec), bf),
        in_specs=[pl.BlockSpec(memory_space=pltpu.HBM)] * 4 + [pl.BlockSpec(memory_space=pl.ANY)] * 3,
        out_specs=vmem,
        scratch_shapes=scratch,
        compiler_params=pltpu.CompilerParams(
            collective_id=0, has_side_effects=True, vmem_limit_bytes=VMEM_LIMIT),
        name="filter_steps",
    )(*[pltpu.with_memory_space_constraint(a, pltpu.HBM) for a in (start_vectors, tiles, tile_rows, tile_cols)],
      tile_counts, center, half_width)


VMEM_LIMIT = 56_350_000


def solution(mesh):
    return jax.shard_map(
        per_device,
        mesh=mesh,
        in_specs=(
            P(("row", "col"), None),
            P("row", "col", None, None),
            P("row", "col"),
            P("row", "col"),
            P("row", "col"),
            P(),
            P(),
        ),
        out_specs=P(("row", "col"), None),
        check_vma=False,
    )
```

time: 42.3 us -> 42 us (level)
  no operation moved by 1% of the time
where the time goes in v5:
time: 42 us; the launch traced here: 41.9 us
  Pallas kernels  39.3 us (94%)
  between operations  1.95 us (5%)
  local copies, waits for them, and re-layouts  0.66 us (2%)
    pallas_call x1, Pallas kernels, per_device(): pl.pallas_call(functools.partial(filter_kernel, (R, C, half, pt, slots, v...  39.3 us

profile of v5, /device:TPU:0, one launch (start us, length us, event | category | flops | bytes accessed | tf_op | source)
XLA Modules:
  0.0 41.9 jit_solution(18377389065332084287)
XLA Ops:
  1.9 39.3 %filter_steps.1 = bf16[512,128]{1,0:T(8,128)(2,1)S(1)} custom-call(bf16[512,128]{1,0:T(8,128)(2,1)} %x_ref.1, bf16[1,32,128,128]{3,2,1,0:T(8,128)(2,1)} %tiles_ref.1, s32[1,32]{1,0:T(1,128)} %rows_ref.1, s32[1,32]{1,0:T(1,128)} %cols_ref.1, s32[1,1]{1,0:T(1,128)S(6)} %copy.9.used_ref, f32[1]{0:T(128)S(6)} %copy.10.shift_ref, f32[1]{0:T(128)S(6)} %copy.11.scale_ref), custom_call_target="tpu_custom_call" | custom-call | tf_op jit(solution)/shard_map/filter_steps/pallas_call | solution.py:507
  41.2 0.7 %copy.12 = bf16[512,128]{1,0:T(8,128)(2,1)} copy(bf16[512,128]{1,0:T(8,128)(2,1)S(1)} %filter_steps.1) | data formatting | bytes 262144

commit v6 on v5

--- a/solution.py
+++ b/solution.py
@@ -15,13 +15,13 @@
 UNROLL = 16
 MESH_ID = pl.DeviceIdType.MESH
 GATHER_TREES = ((("tail3",), ("tail3",)), (("tail3",), ("tail3",)))
-REDUCE_TREES = ((("tail",), ("tail",)), (("tail",), ("tail",)))
+REDUCE_TREES = ((("tail3",), ("tail",)), (("tail3",), ("tail",)))
 ORDER = (
-    "GZ000", "GX00", "GZ001", "XF100", "GX01", "GF2S000", "XF200", "D00", "XF101", "XF201",
-    "GF2S001", "D01", "RM1L000", "RM2L000", "B00", "RX00", "RM2L001", "B01", "RM1L001", "RX01",
-    "E00", "GZ010", "GX10", "GF2S010", "E01", "GZ011", "GX11", "XF110", "XF210", "GF2S011",
-    "D10", "XF111", "XF211", "B10", "D11", "RM1L010", "RX10", "RM2L010", "B11", "RM2L011",
-    "RX11", "RM1L011", "E10", "E11",
+    "GX00", "GZ000", "GZ001", "XF200", "GF2S000", "XF100", "GX01", "D00", "GF2S001", "XF101",
+    "XF201", "D01", "RM2L000", "B00", "RX00", "RM2L001", "B01", "RM1L001", "RX01", "E00",
+    "GZ010", "GX10", "GF2S010", "E01", "GZ011", "GX11", "XF110", "GF2S011", "XF210", "D10",
+    "XF111", "XF211", "B10", "RM2L010", "D11", "RX10", "B11", "RM2L011", "RX11", "RM1L011",
+    "E10", "E11",
 )
 SCOPE = contextlib.nullcontext
 
@@ -87,6 +87,23 @@
                         at += bool(users[0] | users[1])
             count = max(count, at)
     return through, count
+
+
+def line_hops(C, K, parts):
+    hops = set()
+    for t in range(2):
+        for h in range(K):
+            for u in range(parts):
+                for n in range(C):
+                    for sgn in (1, -1):
+                        for d in range(1, C):
+                            on = way_at(C, t, h, u, n, sgn, d)
+                            if on is not None:
+                                hops.add(d - on[0])
+                            length = side(C - 1 - n, sgn, C)
+                            if d <= length:
+                                hops.add(d - parent(GATHER_TREES[t][h][u], length, d))
+    return sorted(hops)
 
 
 def parse(word):
@@ -198,16 +215,23 @@
     EVEN, ODD, PAIR, LAST, PIECES = 0, hq, hq + 1, hq + 2, hq + 3
     through, _ = arrivals(C, K, hq, parts)
 
+    load_x = pltpu.make_async_copy(x_ref, x_in, local.at[0])
+    load_x.start()
     barrier = pltpu.get_barrier_semaphore()
     row_peers = sorted({d % R for d in range(2, half + 1, 2)} | {-d % R for d in range(2, half + 1, 2)})
     for off in row_peers:
         pl.semaphore_signal(barrier, inc=1, device_id={"row": lax.rem(r + off, R)}, device_id_type=MESH_ID)
     pl.semaphore_signal(barrier, inc=1, device_id={"row": partner}, device_id_type=MESH_ID)
-    for off in range(1, C):
-        pl.semaphore_signal(barrier, inc=1, device_id={"col": lax.rem(c + off, C)}, device_id_type=MESH_ID)
-
-    load_x = pltpu.make_async_copy(x_ref, x_in, local.at[0])
-    load_x.start()
+    greeted = len(row_peers) + 1
+    for hop in range(1, C):
+        for sgn in (1, -1):
+            cond = among(lambda n: 0 <= n + sgn * hop < C)[1]
+
+            def greet():
+                pl.semaphore_signal(barrier, inc=1, device_id={"col": c + sgn * hop}, device_id_type=MESH_ID)
+            when(cond, greet)
+            greeted += int(cond) if isinstance(cond, bool) else jnp.where(cond, 1, 0)
+
     small = (
         (rows_ref, row_of), (cols_ref, col_of), (used_ref, counts_ref), (shift_ref, center_ref), (scale_ref, width_ref))
     loads = [pltpu.make_async_copy(src, dst, local.at[3 + i]) for i, (src, dst) in enumerate(small)]
@@ -236,16 +260,20 @@
                         def test(n):
                             on = way_on(t, h, u, n - sgn * d, sgn, d)
                             return on is not None and on[0] == 0
-                        members, cond = final[t, h, u, sgn, d] = among(test)
-                        if cond is not True and cond is not False:
-                            def clear():
-                                part_at(col_fin[t][h], way(sgn, d), u)[...] = jnp.zeros(
-                                    (ptu, vcs[h], size), jnp.bfloat16)
-                            pl.when(jnp.logical_not(cond))(clear)
-            tiles_at(pair_in[t][h], hq)[...] = jnp.zeros((pt, vcs[h], size), jnp.bfloat16)
-    for h in range(K):
-        back[h][slots] = jnp.zeros((vcs[h], size), jnp.float32)
-        direct[h][slots] = jnp.zeros((vcs[h], size), jnp.float32)
+                        final[t, h, u, sgn, d] = among(test)
+
+    def clear():
+        for (t, h, u, sgn, d), (_, cond) in final.items():
+            if cond is not True and cond is not False:
+                def zero():
+                    part_at(col_fin[t][h], way(sgn, d), u)[...] = jnp.zeros((ptu, vcs[h], size), jnp.bfloat16)
+                pl.when(jnp.logical_not(cond))(zero)
+        for t in range(2):
+            for h in range(K):
+                tiles_at(pair_in[t][h], hq)[...] = jnp.zeros((pt, vcs[h], size), jnp.bfloat16)
+        for h in range(K):
+            back[h][slots] = jnp.zeros((vcs[h], size), jnp.float32)
+            direct[h][slots] = jnp.zeros((vcs[h], size), jnp.float32)
 
     with SCOPE("loadx"):
         load_x.wait()
@@ -256,7 +284,7 @@
             win[0][h][j] = part
             seg[0][h][c * pt + j] = part
     with SCOPE("greet"):
-        pl.semaphore_wait(barrier, len(row_peers) + 1 + C - 1)
+        pl.semaphore_wait(barrier, greeted)
 
     sends = [0] * C
 
@@ -459,6 +487,7 @@
             first.discard((kind, *args))
             if not first:
                 with SCOPE("link"):
+                    clear()
                     link_slots()
     with SCOPE("out"):
         for j in range(pt):
@@ -517,7 +546,7 @@
       tile_counts, center, half_width)
 
 
-VMEM_LIMIT = 56_350_000
+VMEM_LIMIT = 48 << 20
 
 
 def solution(mesh):

time: 42 us -> 41.8 us (level)
  no operation moved by 1% of the time
where the time goes in v6:
time: 41.8 us; the launch traced here: 41.6 us
  Pallas kernels  39 us (93%)
  between operations  1.95 us (5%)
  local copies, waits for them, and re-layouts  0.66 us (2%)
    pallas_call x1, Pallas kernels, per_device(): pl.pallas_call(functools.partial(filter_kernel, (R, C, half, pt, slots, v...  39 us

profile of v6, /device:TPU:0, one launch (start us, length us, event | category | flops | bytes accessed | tf_op | source)
XLA Modules:
  0.0 41.6 jit_solution(15405352076559753401)
XLA Ops:
  1.9 39.0 %filter_steps.1 = bf16[512,128]{1,0:T(8,128)(2,1)S(1)} custom-call(bf16[512,128]{1,0:T(8,128)(2,1)} %x_ref.1, bf16[1,32,128,128]{3,2,1,0:T(8,128)(2,1)} %tiles_ref.1, s32[1,32]{1,0:T(1,128)} %rows_ref.1, s32[1,32]{1,0:T(1,128)} %cols_ref.1, s32[1,1]{1,0:T(1,128)S(6)} %copy.9.used_ref, f32[1]{0:T(128)S(6)} %copy.10.shift_ref, f32[1]{0:T(128)S(6)} %copy.11.scale_ref), custom_call_target="tpu_custom_call" | custom-call | tf_op jit(solution)/shard_map/filter_steps/pallas_call | solution.py:536
  40.9 0.7 %copy.12 = bf16[512,128]{1,0:T(8,128)(2,1)} copy(bf16[512,128]{1,0:T(8,128)(2,1)S(1)} %filter_steps.1) | data formatting | bytes 262144

commit v7 on v6

--- a/solution.py
+++ b/solution.py
@@ -12,7 +12,7 @@
 CHUNKS = len(SHARES)
 GRAIN = 16
 PARTS = 1
-UNROLL = 16
+UNROLL = 32
 MESH_ID = pl.DeviceIdType.MESH
 GATHER_TREES = ((("tail3",), ("tail3",)), (("tail3",), ("tail3",)))
 REDUCE_TREES = ((("tail3",), ("tail",)), (("tail3",), ("tail",)))

time: 41.8 us -> 41.5 us (level)
  no operation moved by 1% of the time
where the time goes in v7:
time: 41.5 us; the launch traced here: 41.3 us
  Pallas kernels  38.7 us (93%)
  between operations  1.95 us (5%)
  local copies, waits for them, and re-layouts  0.66 us (2%)
    pallas_call x1, Pallas kernels, per_device(): pl.pallas_call(functools.partial(filter_kernel, (R, C, half, pt, slots, v...  38.7 us

profile of v7, /device:TPU:0, one launch (start us, length us, event | category | flops | bytes accessed | tf_op | source)
XLA Modules:
  0.0 41.3 jit_solution(7361222280860549373)
XLA Ops:
  1.9 38.7 %filter_steps.1 = bf16[512,128]{1,0:T(8,128)(2,1)S(1)} custom-call(bf16[512,128]{1,0:T(8,128)(2,1)} %x_ref.1, bf16[1,32,128,128]{3,2,1,0:T(8,128)(2,1)} %tiles_ref.1, s32[1,32]{1,0:T(1,128)} %rows_ref.1, s32[1,32]{1,0:T(1,128)} %cols_ref.1, s32[1,1]{1,0:T(1,128)S(6)} %copy.9.used_ref, f32[1]{0:T(128)S(6)} %copy.10.shift_ref, f32[1]{0:T(128)S(6)} %copy.11.scale_ref), custom_call_target="tpu_custom_call" | custom-call | tf_op jit(solution)/shard_map/filter_steps/pallas_call | solution.py:536
  40.7 0.7 %copy.12 = bf16[512,128]{1,0:T(8,128)(2,1)} copy(bf16[512,128]{1,0:T(8,128)(2,1)S(1)} %filter_steps.1) | data formatting | bytes 262144
